TPU v7x, 32 devices: a whole 2x2x4 slice. The times are simulated.
32 devices in a mesh: ctx: 8 (over z, y), head: 4 (over x, core).
Axes of the slice: x: 2, y: 2, z: 4, core: 2. Of those that a mesh axis runs over, the one named last changes fastest.
Arguments:
- query: bfloat16 [2048, 4096], P('ctx', 'head'), may hold values from -6 to 6
- key: bfloat16 [2048, 4096], P('ctx', 'head'), may hold values from -6 to 6
- value: bfloat16 [2048, 4096], P('ctx', 'head'), may hold values from -6 to 6
- episode_lengths: int32 [8], replicated, may hold values from 1 to 1024, 2048 in all
- attn_gain: float32 [4096], P('head'), may hold values from 0.1 to 1.9
- out_weight: bfloat16 [4096, 3072], P('head', 'ctx'), may hold values from -0.09375 to 0.09375
- residual: bfloat16 [2048, 3072], P('ctx', 'head'), may hold values from -36 to 36
- norm_gain: float32 [3072], P('head'), may hold values from 0.1 to 1.9
- expert_ids: int32 [2048, 2], P('ctx'), may hold values from 0 to 7, all different within a row; in each aligned block of 256 rows (0 to 255, 256 to 511, ...) at most 96 rows name the same one
- route_weights: int32 [2048, 2], P('ctx'), may hold values from 4096 to 65535
- gate_weight: bfloat16 [8, 3072, 5120], P('ctx', None, 'head'), may hold values from -0.109375 to 0.109375
- up_weight: bfloat16 [8, 3072, 5120], P('ctx', None, 'head'), may hold values from -0.109375 to 0.109375
- down_weight: bfloat16 [8, 5120, 3072], P('ctx', 'head'), may hold values from -0.125 to 0.125
Outputs:
- layer_out: bfloat16 [2048, 3072], P('ctx', 'head')
Inputs may be any that keep to these rules, and one draw needn't show every extreme that they name: `expert_ids`: in the rows of one device (256 tokens) no expert is named by more than 96 rows, a bound that some block reaches; a row names two different experts.
All inputs are finite; a program needn't handle non-finite values.
Results may differ from a plain program's by a relative error of at most 0.012.
Values may be sent and summed in bfloat16 or wider, within the bound.
A program may use at most 128 MiB of HBM per device.

v0:
```python
import jax
import jax.numpy as jnp
from jax import lax
from jax.sharding import PartitionSpec as P

HEAD_DIM = 128


highest = lax.Precision.HIGHEST


def entering(value, axis, join, neutral):
    place = lax.axis_index(axis)
    gathered = jax.tree.map(
        lambda a, kind: lax.all_gather(a.astype(kind), axis), value, (jnp.bfloat16, jnp.bfloat16)
    )
    state = jax.tree.map(lambda a, e: jnp.zeros_like(a) + jnp.asarray(e, a.dtype), value, neutral)

    def one(step, state):
        return join(
            state,
            jax.tree.map(
                lambda a, own: lax.dynamic_index_in_dim(a, step, 0, False).astype(own.dtype),
                gathered,
                value,
            ),
        )

    return lax.fori_loop(0, place, one, state)


def episode_of(positions, lengths):
    starts = jnp.cumsum(lengths) - lengths
    return jnp.sum((starts[None, :] <= positions[:, None]).astype(jnp.int32), axis=1) - 1


def link_states(earlier, latter):
    marker = jnp.maximum(earlier[0], latter[0])
    joined = jnp.where(latter[0][0] > 0.0, latter[1], earlier[1] + latter[1])
    return (marker, joined)


def on_device(
    query,
    key,
    value,
    episode_lengths,
    attn_gain,
    out_weight,
    residual,
    norm_gain,
    expert_ids,
    route_weights,
    gate_weight,
    up_weight,
    down_weight,
):
    tok_rows = query.shape[0]
    head_size = HEAD_DIM
    heads_local = query.shape[1] // head_size
    own_index = lax.axis_index("ctx")
    ctx_count = lax.axis_size("ctx")
    positions = own_index * tok_rows + jnp.arange(tok_rows, dtype=jnp.int32)
    episode = episode_of(positions, episode_lengths)
    prior = episode_of(positions[:1] - 1, episode_lengths)[0]
    final = episode[-1]
    lifted_query = jax.nn.silu(query.astype(jnp.float32)).reshape(tok_rows, heads_local, head_size)
    lifted_key = jax.nn.silu(key.astype(jnp.float32)).reshape(tok_rows, heads_local, head_size)
    value_rows = value.astype(jnp.float32).reshape(tok_rows, heads_local, head_size)
    keep = (episode == final).astype(jnp.float32)
    state = jnp.einsum(
        "shd,she->hde", lifted_key * keep[:, None, None], value_rows, precision=highest
    )
    marker = (final != prior).astype(jnp.float32).reshape(1)
    blank = (jnp.zeros((1,), jnp.float32), jnp.zeros_like(state))
    carried = entering((marker, state), "ctx", link_states, blank)
    carry_state = carried[1]
    order = jnp.arange(tok_rows, dtype=jnp.int32)
    allowed = ((order[:, None] >= order[None, :]) & (episode[:, None] == episode[None, :])).astype(
        jnp.float32
    )
    scores = jnp.einsum("thd,shd->hts", lifted_query, lifted_key, precision=highest)
    inside = jnp.einsum("hts,shd->thd", scores * allowed[None], value_rows, precision=highest)
    outside = jnp.einsum("thd,hde->the", lifted_query, carry_state, precision=highest)
    attn = inside + outside * (episode == prior).astype(jnp.float32)[:, None, None]
    mean_square = jnp.mean(attn * attn, axis=2, keepdims=True)
    scaled = attn * lax.rsqrt(mean_square + 1e-06) * attn_gain.reshape(heads_local, head_size)
    headed = scaled.reshape(tok_rows, heads_local * head_size).astype(jnp.bfloat16)
    mixed_part = jnp.dot(
        headed,
        lax.all_gather(out_weight, "ctx", axis=1, tiled=True),
        preferred_element_type=jnp.float32,
    )
    width = mixed_part.shape[1]
    mixed_slice = lax.psum_scatter(
        mixed_part.astype(jnp.bfloat16), "head", scatter_dimension=1, tiled=True
    ).astype(jnp.float32)
    hidden_slice = residual.astype(jnp.float32) + mixed_slice
    squares = lax.psum(jnp.sum(hidden_slice * hidden_slice, axis=1), "head")
    normed = (hidden_slice * lax.rsqrt(squares / width + 1e-06)[:, None] * norm_gain).astype(
        jnp.bfloat16
    )
    experts_count = gate_weight.shape[0] * ctx_count
    capacity = 3 * tok_rows // experts_count
    flat_ids = expert_ids.reshape(-1)
    onehot = (flat_ids[:, None] == jnp.arange(experts_count, dtype=jnp.int32)[None, :]).astype(
        jnp.int32
    )
    slot = jnp.sum(jnp.cumsum(onehot, axis=0) * onehot, axis=1) - 1
    source_rows = jnp.repeat(normed, 2, axis=0)
    outgoing = (
        jnp.zeros((experts_count, capacity, normed.shape[1]), jnp.bfloat16)
        .at[flat_ids, slot]
        .set(source_rows)
    )
    raw_weights = route_weights.astype(jnp.float32)
    share = (raw_weights / jnp.sum(raw_weights, axis=1, keepdims=True)).reshape(-1)
    full_rows = lax.all_gather(
        lax.all_to_all(outgoing, "ctx", split_axis=0, concat_axis=0, tiled=True),
        "head",
        axis=2,
        tiled=True,
    )
    flat = full_rows.reshape(-1, full_rows.shape[2])
    gate = jnp.dot(flat, gate_weight[0], preferred_element_type=jnp.float32)
    up = jnp.dot(flat, up_weight[0], preferred_element_type=jnp.float32)
    gated = (jax.nn.silu(gate) * up).astype(jnp.bfloat16)
    partial_value = jnp.dot(gated, down_weight[0], preferred_element_type=jnp.float32).astype(
        jnp.bfloat16
    )
    answer_partial_value = partial_value.reshape(
        full_rows.shape[0], full_rows.shape[1], partial_value.shape[1]
    )
    returned = lax.all_to_all(answer_partial_value, "ctx", split_axis=0, concat_axis=0, tiled=True)
    picked = returned[flat_ids, slot].astype(jnp.float32)
    weighted = jnp.sum((picked * share[:, None]).reshape(tok_rows, 2, picked.shape[1]), axis=1)
    moe = lax.psum_scatter(
        weighted.astype(jnp.bfloat16), "head", scatter_dimension=1, tiled=True
    ).astype(jnp.float32)
    return (hidden_slice + moe).astype(jnp.bfloat16)


def solution(mesh):
    placed = (
        P("ctx", "head"),
        P("ctx", "head"),
        P("ctx", "head"),
        P(),
        P("head"),
        P("head", "ctx"),
        P("ctx", "head"),
        P("head"),
        P("ctx", None),
        P("ctx", None),
        P("ctx", None, "head"),
        P("ctx", None, "head"),
        P("ctx", "head", None),
    )
    return jax.shard_map(
        on_device, mesh=mesh, in_specs=placed, out_specs=P("ctx", "head"), check_vma=False
    )
```

profile of v0, /device:TPU:0, one launch (start us, length us, event | category | flops | bytes accessed | tf_op | source)
XLA Modules:
  0.0 522.1 jit_solution(17571287380999060670)
XLA Ops:
  7.7 0.8 reduce-window.19
  8.6 1.3 fusion.50
  10.5 1.3 convert_multiply_fusion
  12.8 0.6 compare_convert_fusion
  13.4 1.4 convolution_convert_fusion.1
  14.9 0.7 all-gather.5.cloned.1.call-update
  16.2 0.6 dynamic-slice
  16.8 0.7 dynamic-update-slice
  17.5 23.2 %all-reduce = bf16[8]{0:T(256)(128)(2,1)S(1)} all-reduce(bf16[8]{0:T(256)(128)(2,1)S(1)} %dynamic-update-slice), channel_id=1, replica_groups=mesh['ctx'=8,'head'=4] {'ctx'}, use_global_device_ids=true, to_apply=%add | all-reduce | flops 8 | bytes 32
  40.9 3.4 fusion.32
  44.3 22.6 %all-gather.9.cloned.1.call-done = bf16[64,128,128]{2,1,0:T(8,128)(2,1)} async-done(((bf16[8,128,128]{2,1,0:T(8,128)(2,1)}), bf16[64,128,128]{2,1,0:T(8,128)(2,1)}) %all-gather.9.cloned.1.call-update) | async-done | bytes 2097168 | tf_op jit(solution)/shard_map/all_gather | solution.py:15
  67.0 1.3 fusion.23
  68.6 1.5 multiply_reduce_fusion.1
  70.3 96.8 %all-gather.5.cloned.1.call-done = bf16[1024,3072]{1,0:T(8,128)(2,1)} async-done(((bf16[1024,384]{1,0:T(8,128)(2,1)}), bf16[1024,3072]{1,0:T(8,128)(2,1)}) %all-gather.5.cloned.1.call-update) | async-done | bytes 6291472 | tf_op jit(solution)/shard_map/all_gather | solution.py:91
  167.0 5.8 %convolution_convert_fusion = bf16[256,3072]{1,0:T(8,128)(2,1)} fusion(bf16[256,1024]{0,1:T(8,128)(2,1)S(1)} %bitcast.92, bf16[1024,3072]{1,0:T(8,128)(2,1)} %all-gather.5.cloned.1.call-done), kind=kOutput, calls=%fused_computation.13 | convolution fusion | flops 1611399168 | bytes 8388608 | tf_op jit(solution)/shard_map/dot_general | solution.py:89
  173.5 1.1 reduce-window.20
  175.0 24.2 %reduce-scatter.3.cloned.1.call-done = bf16[256,768]{1,0:T(8,128)(2,1)} async-done(((bf16[256,3072]{1,0:T(8,128)(2,1)}), bf16[256,768]{1,0:T(8,128)(2,1)}) %reduce-scatter.3.cloned.1.call-update) | async-done | bytes 393232 | tf_op jit(solution)/shard_map/reduce_scatter | solution.py:95
  199.3 1.2 multiply_reduce_fusion.2
  200.5 5.8 %psum.7 = f32[256]{0:T(256)S(1)} all-reduce(f32[256]{0:T(256)S(1)} %multiply_reduce_fusion.2), channel_id=1, replica_groups=mesh['ctx'=8,'head'=4] {'head'}, use_global_device_ids=true, to_apply=%region_11.12 | all-reduce | flops 256 | bytes 2048 | tf_op jit(solution)/shard_map/psum | solution.py:99
  206.2 1.2 multiply_convert_fusion.1
  208.2 30.3 %scatter_fusion = bf16[8,96,768]{2,1,0:T(8,128)(2,1)S(1)} fusion(bf16[8,96,768]{2,1,0:T(8,128)(2,1)S(1)} %broadcast_in_dim.7, s32[512]{0:T(512)S(1)} %bitcast.88, bf16[512,768]{1,0:T(8,128)(2,1)S(1)} %reshape.237), kind=kCustom, calls=%fused_computation.1 | custom fusion | bytes 2363392 | tf_op jit(solution)/shard_map/scatter | solution.py:114
  238.5 34.5 %all_to_all.10 = bf16[8,96,768]{2,1,0:T(8,128)(2,1)} all-to-all(bf16[8,96,768]{2,1,0:T(8,128)(2,1)S(1)} %scatter_fusion), channel_id=1, replica_groups=mesh['ctx'=8,'head'=4] {'ctx'}, dimensions={0} | all-to-all | bytes 2359296 | tf_op jit(solution)/shard_map/all_to_all | solution.py:119
  273.0 35.3 %all-gather.7.cloned.1.call-done = bf16[8,96,3072]{2,1,0:T(8,128)(2,1)} async-done(((bf16[8,96,768]{2,1,0:T(8,128)(2,1)}), bf16[8,96,3072]{2,1,0:T(8,128)(2,1)}) %all-gather.7.cloned.1.call-update) | async-done | bytes 4718608 | tf_op jit(solution)/shard_map/all_gather | solution.py:118
  308.3 11.7 %fusion.4 = f32[768,1280]{1,0:T(8,128)} fusion(bf16[768,3072]{1,0:T(8,128)(2,1)} %bitcast.98, bf16[1,3072,1280]{2,1,0:T(8,128)(2,1)} %param.25), kind=kOutput, calls=%fused_computation.8 | convolution fusion | flops 6039797760 | bytes 16515072 | tf_op jit(solution)/shard_map/dot_general | solution.py:125
  320.0 22.0 %fusion.6 = bf16[768,3072]{1,0:T(8,128)(2,1)} fusion(bf16[1,1280,3072]{2,1,0:T(8,128)(2,1)} %param.27, bf16[768,3072]{1,0:T(8,128)(2,1)} %bitcast.99, bf16[1,3072,1280]{2,1,0:T(8,128)(2,1)} %param.26, f32[768,1280]{1,0:T(8,128)} %fusion.4), kind=kOutput, calls=%fused_computation.11 | convolution fusion | flops 12087853056 | bytes 29097984 | tf_op jit(solution)/shard_map/dot_general | solution.py:128
  342.1 5.6 %all-to-all-start.1 = ((bf16[8,96,3072]{2,1,0:T(8,128)(2,1)}), bf16[8,96,3072]{2,1,0:T(8,128)(2,1)}, u32[]{:S(2)}, u32[]{:S(2)}) async-start(bf16[8,96,3072]{2,1,0:T(8,128)(2,1)} %bitcast.89), calls=%async_computation.2 | async-start | bytes 9437184 | tf_op jit(solution)/shard_map/all_to_all | solution.py:134
  348.2 104.5 %all-to-all-done.1 = bf16[8,96,3072]{2,1,0:T(8,128)(2,1)} async-done(((bf16[8,96,3072]{2,1,0:T(8,128)(2,1)}), bf16[8,96,3072]{2,1,0:T(8,128)(2,1)}, u32[]{:S(2)}, u32[]{:S(2)}) %all-to-all-start.1) | async-done | bytes 4718624 | tf_op jit(solution)/shard_map/all_to_all | solution.py:134
  452.7 15.2 %gather_fusion = bf16[512,3072]{1,0:T(8,128)(2,1)} fusion(bf16[8,96,3072]{2,1,0:T(8,128)(2,1)} %all-to-all-done.1, s32[512]{0:T(512)S(1)} %bitcast.87), kind=kCustom, calls=%fused_computation | custom fusion | bytes 6295552 | tf_op jit(solution)/shard_map/gather | solution.py:135
  467.9 7.8 %reshape.228 = f32[256,2,3072]{2,1,0:T(2,128)} reshape(bf16[512,3072]{1,0:T(8,128)(2,1)} %gather_fusion) | data formatting | bytes 9437184 | tf_op jit(solution)/shard_map/convert_element_type | solution.py:135
  475.7 11.5 %multiply_reduce_fusion = bf16[256,3072]{1,0:T(8,128)(2,1)} fusion(f32[256,2,3072]{2,1,0:T(2,128)} %reshape.228, f32[256,2]{1,0:T(8,128)S(1)} %copy.50), kind=kLoop, calls=%fused_computation.10 | loop fusion | flops 2359296 | bytes 7866368 | tf_op jit(solution)/shard_map/reduce_sum | solution.py:136
  487.2 26.4 %reduce-scatter.5.cloned.1.call-done = bf16[256,768]{1,0:T(8,128)(2,1)} async-done(((bf16[256,3072]{1,0:T(8,128)(2,1)}), bf16[256,768]{1,0:T(8,128)(2,1)}) %reduce-scatter.5.cloned.1.call-update) | async-done | bytes 393232 | tf_op jit(solution)/shard_map/reduce_scatter | solution.py:137
  513.6 1.9 add_convert_fusion
  (61 shorter events, 4.5 us)
Async XLA Ops:
  6.5 6.9 %copy-start = (bf16[256,1024]{1,0:T(8,128)(2,1)S(1)}, bf16[256,1024]{1,0:T(8,128)(2,1)}, u32[]{:S(2)}) copy-start(bf16[256,1024]{1,0:T(8,128)(2,1)} %param.17) | copy-start | bytes 1572868
  6.5 9.7 %copy-start.10 = (u32[32]{0:T(128)S(1)}, u32[32]{0:T(128)}, u32[]{:S(2)}) copy-start(u32[32]{0:T(128)} %constant.109) | copy-start | bytes 388
  6.5 34.3 %copy-start.9 = (bf16[256,1024]{1,0:T(8,128)(2,1)S(1)}, bf16[256,1024]{1,0:T(8,128)(2,1)}, u32[]{:S(2)}) copy-start(bf16[256,1024]{1,0:T(8,128)(2,1)} %param.15) | copy-start | bytes 1572868
  6.5 60.4 %all-gather.9.cloned.1.call-start = ((), (), s32[]{:S(2)}) async-start(), calls=%async_computation.8 | async-start | bytes 2359296 | tf_op jit(solution)/shard_map/all_gather | solution.py:15
  14.8 152.2 %all-gather.5.cloned.1.call-start = ((), (), s32[]{:S(2)}) async-start(), calls=%async_computation.4 | async-start | bytes 7077888 | tf_op jit(solution)/shard_map/all_gather | solution.py:91
  15.6 183.7 %reduce-scatter.3.cloned.1.call-start = ((), (), s32[]{:S(2)}) async-start(), calls=%async_computation.5 | async-start | bytes 1966080 | tf_op jit(solution)/shard_map/reduce_scatter | solution.py:95
  67.0 1.6 copy-start.4
  67.0 3.1 copy-start.6
  167.0 5.9 %copy-start.8 = (s32[256,2]{0,1:T(2,128)S(1)}, s32[256,2]{0,1:T(2,128)}, u32[]{:S(2)}) copy-start(s32[256,2]{0,1:T(2,128)} %param.23) | copy-start | bytes 6148
  167.0 32.2 %copy-start.2 = (bf16[256,768]{1,0:T(8,128)(2,1)S(1)}, bf16[256,768]{1,0:T(8,128)(2,1)}, u32[]{:S(2)}) copy-start(bf16[256,768]{1,0:T(8,128)(2,1)} %param.21) | copy-start | bytes 1179652
  167.0 39.2 %copy-start.7 = (f32[768]{0:T(1024)S(1)}, f32[768]{0:T(1024)}, u32[]{:S(2)}) copy-start(f32[768]{0:T(1024)} %param.22) | copy-start | bytes 9220
  172.9 135.4 %all-gather.7.cloned.1.call-start = ((), (), s32[]{:S(2)}) async-start(), calls=%async_computation.6 | async-start | bytes 5898240 | tf_op jit(solution)/shard_map/all_gather | solution.py:118
  342.1 5.9 %copy-start.5 = (s32[256,2]{0,1:T(2,128)S(1)}, s32[256,2]{0,1:T(2,128)}, u32[]{:S(2)}) copy-start(s32[256,2]{0,1:T(2,128)} %param.24) | copy-start | bytes 6148
  342.1 110.6 %all-to-all-start.1 = ((bf16[8,96,3072]{2,1,0:T(8,128)(2,1)}), bf16[8,96,3072]{2,1,0:T(8,128)(2,1)}, u32[]{:S(2)}, u32[]{:S(2)}) async-start(bf16[8,96,3072]{2,1,0:T(8,128)(2,1)} %bitcast.89), calls=%async_computation.2 | async-start | bytes 9437184 | tf_op jit(solution)/shard_map/all_to_all | solution.py:134
  347.7 165.9 %reduce-scatter.5.cloned.1.call-start = ((), (), s32[]{:S(2)}) async-start(), calls=%async_computation.7 | async-start | bytes 1966080 | tf_op jit(solution)/shard_map/reduce_scatter | solution.py:137
  467.9 47.7 %copy-start.1 = (bf16[256,1024]{1,0:T(8,128)(2,1)S(1)}, bf16[256,1024]{1,0:T(8,128)(2,1)}, u32[]{:S(2)}) copy-start(bf16[256,1024]{1,0:T(8,128)(2,1)} %param.17) | copy-start | bytes 1572868
  475.7 37.9 %copy-start.3 = (bf16[256,768]{1,0:T(8,128)(2,1)S(1)}, bf16[256,768]{1,0:T(8,128)(2,1)}, u32[]{:S(2)}) copy-start(bf16[256,768]{1,0:T(8,128)(2,1)} %reduce-scatter.3.cloned.1.call-done) | copy-start | bytes 1179652
Sparse Core Ops, SparseCore 0:
  14.9 51.9 all-gather.8
  69.0 98.0 all-gather.4
  173.0 26.2 reduce-scatter.2
  273.1 35.1 all-gather.6
  487.4 26.2 reduce-scatter.4
where the time goes:
time: 523 us; the launch traced here: 522 us
  waiting for transfers between devices  311 us (59%)
  blocking collectives  63.5 us (12%)
  local copies, waits for them, and re-layouts  58.1 us (11%)
  matrix products  47.1 us (9%)
  other arithmetic  21.6 us (4%)
  between operations  15.2 us (3%)
  starting transfers between devices  6.03 us (1%)
    all_to_all x1, waiting for transfers between devices, on_device(): lax.all_to_all(answer_partial_value, 'ctx', split_axis=0, concat_axis=0,...  104 us
    all_gather x1, waiting for transfers between devices, on_device(): lax.all_gather(out_weight, 'ctx', axis=1, tiled=True)  96.8 us
    all_gather x1, waiting for transfers between devices, on_device(): lax.all_gather(lax.all_to_all(outgoing, 'ctx', split_axis=0, concat_axis=...  35.3 us
    all_to_all x1, blocking collectives, on_device(): lax.all_to_all(outgoing, 'ctx', split_axis=0, concat_axis=0, tiled=True)  34.5 us
    scatter x1, local copies, waits for them, and re-layouts, on_device(): outgoing = jnp.zeros((experts_count, capacity, normed.shape[1]), jnp.bflo...  30.3 us
    reduce_scatter x1, waiting for transfers between devices, on_device(): lax.psum_scatter(weighted.astype(jnp.bfloat16), 'head', scatter_dimension...  26.4 us
    reduce_scatter x1, waiting for transfers between devices, on_device(): lax.psum_scatter(mixed_part.astype(jnp.bfloat16), 'head', scatter_dimensi...  24.2 us
    unnamed x1, blocking collectives  23.2 us
  transfers between devices with their start and end apart: 6, of which 6 were waited for; matrix products, arithmetic and copies ran while one was open for 2% of the time, Pallas kernels for 0%

commit v1 on v0

--- a/solution.py
+++ b/solution.py
@@ -9,35 +9,9 @@
 highest = lax.Precision.HIGHEST
 
 
-def entering(value, axis, join, neutral):
-    place = lax.axis_index(axis)
-    gathered = jax.tree.map(
-        lambda a, kind: lax.all_gather(a.astype(kind), axis), value, (jnp.bfloat16, jnp.bfloat16)
-    )
-    state = jax.tree.map(lambda a, e: jnp.zeros_like(a) + jnp.asarray(e, a.dtype), value, neutral)
-
-    def one(step, state):
-        return join(
-            state,
-            jax.tree.map(
-                lambda a, own: lax.dynamic_index_in_dim(a, step, 0, False).astype(own.dtype),
-                gathered,
-                value,
-            ),
-        )
-
-    return lax.fori_loop(0, place, one, state)
-
-
 def episode_of(positions, lengths):
     starts = jnp.cumsum(lengths) - lengths
     return jnp.sum((starts[None, :] <= positions[:, None]).astype(jnp.int32), axis=1) - 1
-
-
-def link_states(earlier, latter):
-    marker = jnp.maximum(earlier[0], latter[0])
-    joined = jnp.where(latter[0][0] > 0.0, latter[1], earlier[1] + latter[1])
-    return (marker, joined)
 
 
 def on_device(
@@ -71,10 +45,14 @@
     state = jnp.einsum(
         "shd,she->hde", lifted_key * keep[:, None, None], value_rows, precision=highest
     )
-    marker = (final != prior).astype(jnp.float32).reshape(1)
-    blank = (jnp.zeros((1,), jnp.float32), jnp.zeros_like(state))
-    carried = entering((marker, state), "ctx", link_states, blank)
-    carry_state = carried[1]
+    finals = episode_of(
+        (jnp.arange(ctx_count, dtype=jnp.int32) + 1) * tok_rows - 1, episode_lengths
+    )
+    earlier = (jnp.arange(ctx_count) < own_index) & (finals == prior)
+    gathered = lax.all_gather(state.astype(jnp.bfloat16), "ctx")
+    carry_state = jnp.sum(
+        jnp.where(earlier[:, None, None, None], gathered.astype(jnp.float32), 0.0), axis=0
+    )
     order = jnp.arange(tok_rows, dtype=jnp.int32)
     allowed = ((order[:, None] >= order[None, :]) & (episode[:, None] == episode[None, :])).astype(
         jnp.float32
@@ -107,14 +85,18 @@
         jnp.int32
     )
     slot = jnp.sum(jnp.cumsum(onehot, axis=0) * onehot, axis=1) - 1
-    source_rows = jnp.repeat(normed, 2, axis=0)
+    target = (flat_ids * capacity + slot).reshape(tok_rows, 2)
+    places = jnp.arange(experts_count * capacity, dtype=jnp.int32)
+    spread = (
+        (places[:, None] == target[None, :, 0]) | (places[:, None] == target[None, :, 1])
+    ).astype(jnp.bfloat16)
     outgoing = (
-        jnp.zeros((experts_count, capacity, normed.shape[1]), jnp.bfloat16)
-        .at[flat_ids, slot]
-        .set(source_rows)
+        jnp.dot(spread, normed, preferred_element_type=jnp.float32)
+        .astype(jnp.bfloat16)
+        .reshape(experts_count, capacity, normed.shape[1])
     )
     raw_weights = route_weights.astype(jnp.float32)
-    share = (raw_weights / jnp.sum(raw_weights, axis=1, keepdims=True)).reshape(-1)
+    share = raw_weights / jnp.sum(raw_weights, axis=1, keepdims=True)
     full_rows = lax.all_gather(
         lax.all_to_all(outgoing, "ctx", split_axis=0, concat_axis=0, tiled=True),
         "head",
@@ -128,15 +110,16 @@
     partial_value = jnp.dot(gated, down_weight[0], preferred_element_type=jnp.float32).astype(
         jnp.bfloat16
     )
-    answer_partial_value = partial_value.reshape(
-        full_rows.shape[0], full_rows.shape[1], partial_value.shape[1]
-    )
-    returned = lax.all_to_all(answer_partial_value, "ctx", split_axis=0, concat_axis=0, tiled=True)
-    picked = returned[flat_ids, slot].astype(jnp.float32)
-    weighted = jnp.sum((picked * share[:, None]).reshape(tok_rows, 2, picked.shape[1]), axis=1)
-    moe = lax.psum_scatter(
-        weighted.astype(jnp.bfloat16), "head", scatter_dimension=1, tiled=True
-    ).astype(jnp.float32)
+    summed = lax.psum_scatter(partial_value, "head", scatter_dimension=1, tiled=True)
+    answer = summed.reshape(full_rows.shape[0], full_rows.shape[1], summed.shape[1])
+    returned = lax.all_to_all(answer, "ctx", split_axis=0, concat_axis=0, tiled=True)
+    returned = returned.reshape(-1, returned.shape[2])
+    moe = 0.0
+    for k in range(2):
+        pick = (target[:, k : k + 1] == places[None, :]).astype(jnp.bfloat16)
+        moe = moe + share[:, k : k + 1] * jnp.dot(
+            pick, returned, preferred_element_type=jnp.float32
+        )
     return (hidden_slice + moe).astype(jnp.bfloat16)
 
 

time: 523 us -> 402 us (0.77)
  local copies, waits for them, and re-layouts: 58.1 us -> 2.34 us
  waiting for transfers between devices: 311 us -> 279 us
  blocking collectives: 63.5 us -> 40.1 us
  other arithmetic: 21.6 us -> 9.59 us
    all_to_all x1, waiting for transfers between devices: 104 us -> 28.4 us  [on_device(): lax.all_to_all(answer, 'ctx', split_axis=0, concat_axis=0, tiled=True)]
    scatter x1 -> x0, local copies, waits for them, and re-layouts: 30.3 us -> none  [on_device(): outgoing = jnp.zeros((experts_count, capacity, normed.shape[1]), jnp.bflo...]
    all_gather x1, waiting for transfers between devices: 22.6 us -> 47.4 us  [on_device(): gathered = lax.all_gather(state.astype(jnp.bfloat16), 'ctx')]
    unnamed x1 -> x0, blocking collectives: 23.2 us -> none
    reduce_scatter x1, waiting for transfers between devices: 26.4 us -> 48 us  [on_device(): lax.psum_scatter(partial_value, 'head', scatter_dimension=1, tiled=True)]
    gather x1 -> x0, local copies, waits for them, and re-layouts: 15.2 us -> none  [on_device(): picked = returned[flat_ids, slot].astype(jnp.float32)]
    reduce_sum x2, other arithmetic: 11.5 us -> 2.29 us  [the longest x1 2.27 us: on_device(): jnp.sum(jnp.where(earlier[:, None, None, None], gathered.astype(jnp.float...]
    convert_element_type x1 -> x0, local copies, waits for them, and re-layouts: 7.83 us -> none  [on_device(): picked = returned[flat_ids, slot].astype(jnp.float32)]
  transfers between devices with their start and end apart: 6 -> 6, of which waited for: 6 -> 6; matrix products, arithmetic and copies ran while one was open for 2% -> 3% of each run, Pallas kernels for 0% -> 0%
where the time goes in v1:
time: 402 us
  waiting for transfers between devices  279 us (69%)
  matrix products  50.6 us (13%)
  blocking collectives  40.1 us (10%)
  between operations  14.7 us (4%)
  other arithmetic  9.59 us (2%)
  starting transfers between devices  5.86 us (1%)
    all_gather x1, waiting for transfers between devices, on_device(): lax.all_gather(out_weight, 'ctx', axis=1, tiled=True)  94.8 us
    reduce_scatter x1, waiting for transfers between devices, on_device(): lax.psum_scatter(partial_value, 'head', scatter_dimension=1, tiled=True)  48 us
    all_gather x1, waiting for transfers between devices, on_device(): gathered = lax.all_gather(state.astype(jnp.bfloat16), 'ctx')  47.4 us
    all_gather x1, waiting for transfers between devices, on_device(): lax.all_gather(lax.all_to_all(outgoing, 'ctx', split_axis=0, concat_axis=...  35.1 us
    all_to_all x1, blocking collectives, on_device(): lax.all_to_all(outgoing, 'ctx', split_axis=0, concat_axis=0, tiled=True)  34.3 us
    all_to_all x1, waiting for transfers between devices, on_device(): lax.all_to_all(answer, 'ctx', split_axis=0, concat_axis=0, tiled=True)  28.4 us
    reduce_scatter x1, waiting for transfers between devices, on_device(): lax.psum_scatter(mixed_part.astype(jnp.bfloat16), 'head', scatter_dimensi...  24.1 us
    dot_general x1, matrix products, on_device(): jnp.dot(gated, down_weight[0], preferred_element_type=jnp.float32)  22 us
  transfers between devices with their start and end apart: 6, of which 6 were waited for; matrix products, arithmetic and copies ran while one was open for 3% of the time, Pallas kernels for 0%

profile of v1, /device:TPU:0, one launch (start us, length us, event | category | flops | bytes accessed | tf_op | source)
XLA Modules:
  0.0 401.7 jit_solution(13591992474148500352)
XLA Ops:
  6.5 0.5 slice.26
  7.7 0.8 reduce-window.19
  8.5 1.4 fusion.61
  10.0 0.6 slice.27
  10.6 1.3 convert_multiply_fusion
  11.9 0.3 copy.69
  13.0 0.7 compare_convert_fusion
  13.6 1.4 convolution_convert_fusion.2
  15.1 0.7 all-gather.5.cloned.1.call-update
  16.1 3.4 fusion.36
  19.6 47.4 %all-gather.9.cloned.1.call-done = bf16[64,128,128]{2,1,0:T(8,128)(2,1)} async-done(((bf16[8,128,128]{2,1,0:T(8,128)(2,1)}), bf16[64,128,128]{2,1,0:T(8,128)(2,1)}) %all-gather.9.cloned.1.call-update) | async-done | bytes 2097168 | tf_op jit(solution)/shard_map/all_gather | solution.py:52
  67.0 2.3 fusion.12
  69.3 1.3 fusion.24
  70.6 1.5 multiply_reduce_fusion
  72.1 0.2 multiply_convert_fusion
  72.3 94.8 %all-gather.5.cloned.1.call-done = bf16[1024,3072]{1,0:T(8,128)(2,1)} async-done(((bf16[1024,384]{1,0:T(8,128)(2,1)}), bf16[1024,3072]{1,0:T(8,128)(2,1)}) %all-gather.5.cloned.1.call-update) | async-done | bytes 6291472 | tf_op jit(solution)/shard_map/all_gather | solution.py:69
  167.1 5.8 %convolution_convert_fusion = bf16[256,3072]{1,0:T(8,128)(2,1)} fusion(bf16[256,1024]{0,1:T(8,128)(2,1)S(1)} %bitcast.85, bf16[1024,3072]{1,0:T(8,128)(2,1)} %all-gather.5.cloned.1.call-done), kind=kOutput, calls=%fused_computation.10 | convolution fusion | flops 1611399168 | bytes 8388608 | tf_op jit(solution)/shard_map/dot_general | solution.py:67
  173.4 1.1 reduce-window.20
  175.2 24.1 %reduce-scatter.3.cloned.1.call-done = bf16[256,768]{1,0:T(8,128)(2,1)} async-done(((bf16[256,3072]{1,0:T(8,128)(2,1)}), bf16[256,768]{1,0:T(8,128)(2,1)}) %reduce-scatter.3.cloned.1.call-update) | async-done | bytes 393232 | tf_op jit(solution)/shard_map/reduce_scatter | solution.py:73
  199.3 1.2 multiply_reduce_fusion.1
  200.5 5.8 %psum.7 = f32[256]{0:T(256)S(1)} all-reduce(f32[256]{0:T(256)S(1)} %multiply_reduce_fusion.1), channel_id=1, replica_groups=mesh['ctx'=8,'head'=4] {'head'}, use_global_device_ids=true, to_apply=%region_12.13 | all-reduce | flops 256 | bytes 2048 | tf_op jit(solution)/shard_map/psum | solution.py:77
  206.3 1.6 convolution_convert_fusion.1
  207.9 34.3 %all_to_all.10 = bf16[8,96,768]{2,1,0:T(8,128)(2,1)} all-to-all(bf16[8,96,768]{2,1,0:T(8,128)(2,1)S(1)} %bitcast.88), channel_id=1, replica_groups=mesh['ctx'=8,'head'=4] {'ctx'}, dimensions={0} | all-to-all | bytes 2359296 | tf_op jit(solution)/shard_map/all_to_all | solution.py:101
  242.2 0.2 reduce-scatter.5.cloned.1.call-start
  242.5 35.1 %all-gather.7.cloned.1.call-done = bf16[8,96,3072]{2,1,0:T(8,128)(2,1)} async-done(((bf16[8,96,768]{2,1,0:T(8,128)(2,1)}), bf16[8,96,3072]{2,1,0:T(8,128)(2,1)}) %all-gather.7.cloned.1.call-update) | async-done | bytes 4718608 | tf_op jit(solution)/shard_map/all_gather | solution.py:100
  277.6 11.7 %fusion.4 = f32[768,1280]{1,0:T(8,128)} fusion(bf16[768,3072]{1,0:T(8,128)(2,1)} %bitcast.97, bf16[1,3072,1280]{2,1,0:T(8,128)(2,1)} %param.23), kind=kOutput, calls=%fused_computation.4 | convolution fusion | flops 6039797760 | bytes 16515072 | tf_op jit(solution)/shard_map/dot_general | solution.py:107
  289.3 22.0 %fusion.6 = bf16[768,3072]{1,0:T(8,128)(2,1)} fusion(bf16[1,1280,3072]{2,1,0:T(8,128)(2,1)} %param.25, bf16[768,3072]{1,0:T(8,128)(2,1)} %bitcast.98, bf16[1,3072,1280]{2,1,0:T(8,128)(2,1)} %param.24, f32[768,1280]{1,0:T(8,128)} %fusion.4), kind=kOutput, calls=%fused_computation.6 | convolution fusion | flops 12087853056 | bytes 29097984 | tf_op jit(solution)/shard_map/dot_general | solution.py:110
  311.4 48.0 %reduce-scatter.5.cloned.1.call-done = bf16[768,768]{1,0:T(8,128)(2,1)} async-done(((bf16[768,3072]{1,0:T(8,128)(2,1)}), bf16[768,768]{1,0:T(8,128)(2,1)}) %reduce-scatter.5.cloned.1.call-update) | async-done | bytes 1179664 | tf_op jit(solution)/shard_map/reduce_scatter | solution.py:113
  359.4 5.5 %all-to-all-start.1 = ((bf16[8,96,768]{2,1,0:T(8,128)(2,1)}), bf16[8,96,768]{2,1,0:T(8,128)(2,1)S(1)}, u32[]{:S(2)}, u32[]{:S(2)}) async-start(bf16[8,96,768]{2,1,0:T(8,128)(2,1)} %bitcast.87), calls=%async_computation.3 | async-start | bytes 2359296 | tf_op jit(solution)/shard_map/all_to_all | solution.py:115
  364.9 28.4 %all-to-all-done.1 = bf16[8,96,768]{2,1,0:T(8,128)(2,1)S(1)} async-done(((bf16[8,96,768]{2,1,0:T(8,128)(2,1)}), bf16[8,96,768]{2,1,0:T(8,128)(2,1)S(1)}, u32[]{:S(2)}, u32[]{:S(2)}) %all-to-all-start.1) | async-done | bytes 1179680 | tf_op jit(solution)/shard_map/all_to_all | solution.py:115
  393.3 0.5 convolution_multiply_fusion.2
  393.8 1.3 fusion.27
  (50 shorter events, 1.7 us)
Async XLA Ops:
  6.5 7.1 %copy-start = (bf16[256,1024]{1,0:T(8,128)(2,1)S(1)}, bf16[256,1024]{1,0:T(8,128)(2,1)}, u32[]{:S(2)}) copy-start(bf16[256,1024]{1,0:T(8,128)(2,1)} %param.15) | copy-start | bytes 1572868
  6.5 9.6 %copy-start.7 = (bf16[256,1024]{1,0:T(8,128)(2,1)S(1)}, bf16[256,1024]{1,0:T(8,128)(2,1)}, u32[]{:S(2)}) copy-start(bf16[256,1024]{1,0:T(8,128)(2,1)} %param.13) | copy-start | bytes 1572868
  6.5 60.5 %all-gather.9.cloned.1.call-start = ((), (), s32[]{:S(2)}) async-start(), calls=%async_computation.8 | async-start | bytes 2359296 | tf_op jit(solution)/shard_map/all_gather | solution.py:52
  15.0 152.1 %all-gather.5.cloned.1.call-start = ((), (), s32[]{:S(2)}) async-start(), calls=%async_computation.4 | async-start | bytes 7077888 | tf_op jit(solution)/shard_map/all_gather | solution.py:69
  15.8 183.5 %reduce-scatter.3.cloned.1.call-start = ((), (), s32[]{:S(2)}) async-start(), calls=%async_computation.5 | async-start | bytes 1966080 | tf_op jit(solution)/shard_map/reduce_scatter | solution.py:73
  67.0 3.6 copy-start.1
  69.3 2.8 copy-start.6
  167.1 5.9 %copy-start.4 = (s32[256,2]{0,1:T(2,128)S(1)}, s32[256,2]{0,1:T(2,128)}, u32[]{:S(2)}) copy-start(s32[256,2]{0,1:T(2,128)} %param.21) | copy-start | bytes 6148
  167.1 32.2 %copy-start.2 = (bf16[256,768]{1,0:T(8,128)(2,1)S(1)}, bf16[256,768]{1,0:T(8,128)(2,1)}, u32[]{:S(2)}) copy-start(bf16[256,768]{1,0:T(8,128)(2,1)} %param.19) | copy-start | bytes 1179652
  167.1 39.2 %copy-start.8 = (f32[768]{0:T(1024)S(1)}, f32[768]{0:T(1024)}, u32[]{:S(2)}) copy-start(f32[768]{0:T(1024)} %param.20) | copy-start | bytes 9220
  172.9 104.6 %all-gather.7.cloned.1.call-start = ((), (), s32[]{:S(2)}) async-start(), calls=%async_computation.6 | async-start | bytes 5898240 | tf_op jit(solution)/shard_map/all_gather | solution.py:100
  242.2 117.1 %reduce-scatter.5.cloned.1.call-start = ((), (), s32[]{:S(2)}) async-start(), calls=%async_computation.7 | async-start | bytes 5898240 | tf_op jit(solution)/shard_map/reduce_scatter | solution.py:113
  311.4 53.5 %copy-start.5 = (s32[256,2]{0,1:T(2,128)S(1)}, s32[256,2]{0,1:T(2,128)}, u32[]{:S(2)}) copy-start(s32[256,2]{0,1:T(2,128)} %param.22) | copy-start | bytes 6148
  311.4 82.5 %copy-start.3 = (bf16[256,768]{1,0:T(8,128)(2,1)S(1)}, bf16[256,768]{1,0:T(8,128)(2,1)}, u32[]{:S(2)}) copy-start(bf16[256,768]{1,0:T(8,128)(2,1)} %reduce-scatter.3.cloned.1.call-done) | copy-start | bytes 1179652
  359.4 33.9 %all-to-all-start.1 = ((bf16[8,96,768]{2,1,0:T(8,128)(2,1)}), bf16[8,96,768]{2,1,0:T(8,128)(2,1)S(1)}, u32[]{:S(2)}, u32[]{:S(2)}) async-start(bf16[8,96,768]{2,1,0:T(8,128)(2,1)} %bitcast.87), calls=%async_computation.3 | async-start | bytes 2359296 | tf_op jit(solution)/shard_map/all_to_all | solution.py:115
Sparse Core Ops, SparseCore 0:
  15.2 51.7 all-gather.8
  69.1 98.0 all-gather.4
  173.1 26.2 reduce-scatter.2
  242.4 35.1 all-gather.6
  311.5 47.7 reduce-scatter.4

commit v2 on v1

--- a/solution.py
+++ b/solution.py
@@ -1,12 +1,272 @@
+import functools
+
 import jax
 import jax.numpy as jnp
 from jax import lax
+from jax.experimental import pallas as pl
+from jax.experimental.pallas import tpu as pltpu
 from jax.sharding import PartitionSpec as P
 
 HEAD_DIM = 128
 
 
 highest = lax.Precision.HIGHEST
+
+
+MESH = pl.DeviceIdType.MESH
+
+
+def remote(src, dst, send, recv, ctx, head):
+    return pltpu.make_async_remote_copy(
+        src_ref=src,
+        dst_ref=dst,
+        send_sem=send,
+        recv_sem=recv,
+        device_id=(ctx, head),
+        device_id_type=MESH,
+    )
+
+
+def seat():
+    head = lax.axis_index("head")
+    return lax.axis_index("ctx"), lax.div(head, 2), lax.rem(head, 2)
+
+
+def greet(ctx_count, chips, across_ctx):
+    me, chip, core = seat()
+    barrier = pltpu.get_barrier_semaphore()
+
+    def tell(ctx, head):
+        pl.semaphore_signal(barrier, inc=1, device_id=(ctx, head), device_id_type=MESH)
+
+    tell(me, chip * 2 + 1 - core)
+    for j in range(1, chips):
+        tell(me, lax.rem(chip + j, chips) * 2 + core)
+    count = chips
+    if across_ctx:
+
+        @pl.loop(1, ctx_count)
+        def _(i):
+            tell(lax.rem(me + i, ctx_count), chip * 2 + core)
+
+        count += ctx_count - 1
+    pl.semaphore_wait(barrier, count)
+
+
+def dispatch_kernel(
+    n, chips, out_ref, full_ref, here, a_s, a_r, p_s, p_r, x_s, x_r, f_s, f_r
+):
+    me, chip, core = seat()
+    width = out_ref.shape[2]
+    mine, partner = chip * 2 + core, chip * 2 + 1 - core
+
+    def cell(block, head):
+        return full_ref.at[block, :, pl.ds(pl.multiple_of(head * width, 128), width)]
+
+    greet(n, chips, True)
+    own = pltpu.make_async_copy(out_ref.at[me], cell(me, mine), here)
+    own.start()
+
+    def sent(i):
+        to = lax.rem(me + i, n)
+        return remote(out_ref.at[to], cell(me, mine), a_s.at[i], a_r.at[i], to, mine)
+
+    @pl.loop(1, n)
+    def _(i):
+        sent(i).start()
+
+    def block_of(i):
+        return lax.rem(me - i + n, n)
+
+    def arrived(i):
+        return remote(out_ref.at[me], cell(block_of(i), mine), a_s.at[i], a_r.at[i], me, mine)
+
+    def to_partner(i, head):
+        b = cell(block_of(i), head)
+        return remote(b, b, p_s.at[i], p_r.at[i], me, partner)
+
+    def to_chip(i, j):
+        b = cell(block_of(i), mine)
+        return remote(b, b, x_s.at[j, i], x_r.at[j, i], me, lax.rem(chip + j, chips) * 2 + core)
+
+    def from_chip(i, j):
+        b = cell(block_of(i), lax.rem(chip - j + chips, chips) * 2 + core)
+        return remote(b, b, x_s.at[j, i], x_r.at[j, i], me, mine)
+
+    def forward(i, j, which):
+        b = cell(block_of(i), lax.rem(chip - j + chips, chips) * 2 + which)
+        return remote(b, b, f_s.at[j, i], f_r.at[j, i], me, partner)
+
+    def spread(i):
+        for j in range(1, chips):
+            to_chip(i, j).start()
+        to_partner(i, mine).start()
+
+    def relay(i):
+        for j in range(1, chips):
+            from_chip(i, j).wait_recv()
+            forward(i, j, core).start()
+
+    own.wait()
+    spread(0)
+
+    @pl.loop(1, n)
+    def _(i):
+        arrived(i).wait_recv()
+        spread(i)
+
+        @pl.when(i >= 2)
+        def _():
+            relay(i - 2)
+
+    relay(n - 2)
+    relay(n - 1)
+
+    @pl.loop(0, n)
+    def _(i):
+        to_partner(i, partner).wait_recv()
+        to_partner(i, mine).wait_send()
+        for j in range(1, chips):
+            forward(i, j, 1 - core).wait_recv()
+            forward(i, j, core).wait_send()
+            to_chip(i, j).wait_send()
+
+    @pl.loop(1, n)
+    def _(i):
+        sent(i).wait_send()
+
+
+def dispatch(outgoing, n, heads):
+    chips = heads // 2
+    rows, width = outgoing.shape[1:]
+    dma = pltpu.SemaphoreType.DMA
+    return pl.pallas_call(
+        functools.partial(dispatch_kernel, n, chips),
+        out_shape=jax.ShapeDtypeStruct((n, rows, width * heads), outgoing.dtype),
+        in_specs=[pl.BlockSpec(memory_space=pl.ANY)],
+        out_specs=pl.BlockSpec(memory_space=pl.ANY),
+        scratch_shapes=[dma, dma((n,)), dma((n,)), dma((n,)), dma((n,))]
+        + [dma((chips, n))] * 4,
+        compiler_params=pltpu.CompilerParams(collective_id=0, has_side_effects=True),
+        name="dispatch",
+    )(outgoing)
+
+
+def giveback_kernel(
+    n, chips, part_ref, ret_ref, own, pair, out_x, in_x, total, here, l_s, p_s, p_r, x_s, x_r, a_s, a_r
+):
+    me, chip, core = seat()
+    rows, width = ret_ref.shape[1:]
+    mine, partner = chip * 2 + core, chip * 2 + 1 - core
+
+    def cell(block, head):
+        return part_ref.at[block, :, pl.ds(pl.multiple_of(head * width, 128), width)]
+
+    def block_of(i):
+        return lax.rem(me + 1 + i, n)
+
+    def column(j):
+        return lax.rem(chip + j, chips)
+
+    def load(i, j):
+        return pltpu.make_async_copy(
+            cell(block_of(i), column(j) * 2 + core), own.at[i, j], l_s.at[j, i]
+        )
+
+    def swap(i, j):
+        return remote(
+            cell(block_of(i), column(j) * 2 + 1 - core),
+            pair.at[i, j],
+            p_s.at[j, i],
+            p_r.at[j, i],
+            me,
+            partner,
+        )
+
+    def cross(i, j):
+        return remote(
+            out_x.at[i, j], in_x.at[i, j], x_s.at[j, i], x_r.at[j, i], me, column(j) * 2 + core
+        )
+
+    def home(i):
+        return remote(
+            total.at[i], ret_ref.at[me], a_s.at[i], a_r.at[i], block_of(i), mine
+        )
+
+    greet(n, chips, True)
+
+    @pl.loop(0, n)
+    def _(i):
+        for j in list(range(1, chips)) + [0]:
+            swap(i, j).start()
+            load(i, j).start()
+
+    def paired(i, j):
+        load(i, j).wait()
+        swap(i, j).wait_recv()
+        return own[i, j].astype(jnp.float32) + pair[i, j].astype(jnp.float32)
+
+    def first(i):
+        for j in range(1, chips):
+            out_x[i, j] = paired(i, j).astype(jnp.bfloat16)
+            cross(i, j).start()
+
+    def second(i):
+        acc = paired(i, 0)
+        for j in range(1, chips):
+            cross(i, j).wait_recv()
+            acc = acc + in_x[i, j].astype(jnp.float32)
+        total[i] = acc.astype(jnp.bfloat16)
+
+    first(0)
+    first(1)
+
+    @pl.loop(0, n - 1)
+    def _(i):
+        @pl.when(i + 2 < n)
+        def _():
+            first(i + 2)
+
+        second(i)
+        home(i).start()
+
+    second(n - 1)
+    keep = pltpu.make_async_copy(total.at[n - 1], ret_ref.at[me], here)
+    keep.start()
+
+    @pl.loop(0, n - 1)
+    def _(i):
+        back = lax.rem(me - 1 - i + n, n)
+        remote(total.at[i], ret_ref.at[back], a_s.at[i], a_r.at[i], me, mine).wait_recv()
+        home(i).wait_send()
+
+    @pl.loop(0, n)
+    def _(i):
+        for j in range(chips):
+            swap(i, j).wait_send()
+        for j in range(1, chips):
+            cross(i, j).wait_send()
+
+    keep.wait()
+
+
+def giveback(partial_value, n, heads):
+    chips = heads // 2
+    rows, width = partial_value.shape[1], partial_value.shape[2] // heads
+    dma = pltpu.SemaphoreType.DMA
+    piece = pltpu.VMEM((n, chips, rows, width), jnp.bfloat16)
+    return pl.pallas_call(
+        functools.partial(giveback_kernel, n, chips),
+        out_shape=jax.ShapeDtypeStruct((n, rows, width), jnp.bfloat16),
+        in_specs=[pl.BlockSpec(memory_space=pl.ANY)],
+        out_specs=pl.BlockSpec(memory_space=pl.ANY),
+        scratch_shapes=[piece, piece, piece, piece, pltpu.VMEM((n, rows, width), jnp.bfloat16)]
+        + [dma]
+        + [dma((chips, n))] * 5
+        + [dma((n,))] * 2,
+        compiler_params=pltpu.CompilerParams(collective_id=1, has_side_effects=True),
+        name="giveback",
+    )(partial_value)
 
 
 def episode_of(positions, lengths):
@@ -97,12 +357,7 @@
     )
     raw_weights = route_weights.astype(jnp.float32)
     share = raw_weights / jnp.sum(raw_weights, axis=1, keepdims=True)
-    full_rows = lax.all_gather(
-        lax.all_to_all(outgoing, "ctx", split_axis=0, concat_axis=0, tiled=True),
-        "head",
-        axis=2,
-        tiled=True,
-    )
+    full_rows = dispatch(outgoing, ctx_count, lax.axis_size("head"))
     flat = full_rows.reshape(-1, full_rows.shape[2])
     gate = jnp.dot(flat, gate_weight[0], preferred_element_type=jnp.float32)
     up = jnp.dot(flat, up_weight[0], preferred_element_type=jnp.float32)
@@ -110,9 +365,9 @@
     partial_value = jnp.dot(gated, down_weight[0], preferred_element_type=jnp.float32).astype(
         jnp.bfloat16
     )
-    summed = lax.psum_scatter(partial_value, "head", scatter_dimension=1, tiled=True)
-    answer = summed.reshape(full_rows.shape[0], full_rows.shape[1], summed.shape[1])
-    returned = lax.all_to_all(answer, "ctx", split_axis=0, concat_axis=0, tiled=True)
+    returned = giveback(
+        partial_value.reshape(full_rows.shape), ctx_count, lax.axis_size("head")
+    )
     returned = returned.reshape(-1, returned.shape[2])
     moe = 0.0
     for k in range(2):

time: 402 us -> 339 us (0.84)
  waiting for transfers between devices: 279 us -> 167 us
  Pallas kernels: 0 us -> 84 us
  blocking collectives: 40.1 us -> 5.94 us
  starting transfers between devices: 5.86 us -> 0.08 us
    pallas_call x0 -> x2, Pallas kernels: none -> 84 us  [the longest x1 43.6 us: giveback(): pl.pallas_call(functools.partial(giveback_kernel, n, chips), out_shape=ja...]
    reduce_scatter x1 -> x0, waiting for transfers between devices: 48 us -> none  [on_device(): lax.psum_scatter(partial_value, 'head', scatter_dimension=1, tiled=True)]
    all_gather x1 -> x0, waiting for transfers between devices: 35.1 us -> none  [on_device(): lax.all_gather(lax.all_to_all(outgoing, 'ctx', split_axis=0, concat_axis=...]
    all_to_all x1 -> x0, blocking collectives: 34.3 us -> none  [on_device(): lax.all_to_all(outgoing, 'ctx', split_axis=0, concat_axis=0, tiled=True)]
    all_to_all x1 -> x0, waiting for transfers between devices: 28.4 us -> none  [on_device(): lax.all_to_all(answer, 'ctx', split_axis=0, concat_axis=0, tiled=True)]
    all_to_all x1 -> x0, starting transfers between devices: 5.52 us -> none  [on_device(): lax.all_to_all(answer, 'ctx', split_axis=0, concat_axis=0, tiled=True)]
  transfers between devices with their start and end apart: 6 -> 3, of which waited for: 6 -> 3; matrix products, arithmetic and copies ran while one was open for 3% -> 3% of each run, Pallas kernels for 0% -> 0%
where the time goes in v2:
time: 339 us; the launch traced here: 338 us
  waiting for transfers between devices  167 us (49%)
  Pallas kernels  84 us (25%)
  matrix products  54.2 us (16%)
  between operations  14.7 us (4%)
  other arithmetic  9.59 us (3%)
  blocking collectives  5.94 us (2%)
    all_gather x1, waiting for transfers between devices, on_device(): lax.all_gather(out_weight, 'ctx', axis=1, tiled=True)  94.8 us
    all_gather x1, waiting for transfers between devices, on_device(): gathered = lax.all_gather(state.astype(jnp.bfloat16), 'ctx')  47.4 us
    pallas_call x1, Pallas kernels, giveback(): pl.pallas_call(functools.partial(giveback_kernel, n, chips), out_shape=ja...  43.6 us
    pallas_call x1, Pallas kernels, dispatch(): pl.pallas_call(functools.partial(dispatch_kernel, n, chips), out_shape=ja...  40.3 us
    reduce_scatter x1, waiting for transfers between devices, on_device(): lax.psum_scatter(mixed_part.astype(jnp.bfloat16), 'head', scatter_dimensi...  24.1 us
    dot_general x1, matrix products, on_device(): jnp.dot(gated, down_weight[0], preferred_element_type=jnp.float32)  22 us
    dot_general x1, matrix products, on_device(): gate = jnp.dot(flat, gate_weight[0], preferred_element_type=jnp.float32)  11.7 us
  transfers between devices with their start and end apart: 3, of which 3 were waited for; matrix products, arithmetic and copies ran while one was open for 3% of the time, Pallas kernels for 0%

profile of v2, /device:TPU:0, one launch (start us, length us, event | category | flops | bytes accessed | tf_op | source)
XLA Modules:
  0.0 337.8 jit_solution(1536455885331077693)
XLA Ops:
  6.5 0.5 slice.26
  7.7 0.8 reduce-window.19
  8.5 1.4 fusion.61
  10.0 0.6 slice.27
  10.6 1.3 convert_multiply_fusion
  11.9 0.3 copy.69
  13.0 0.7 compare_convert_fusion
  13.6 1.4 convolution_convert_fusion.2
  15.1 0.7 all-gather.4.cloned.1.call-update
  15.8 0.2 convert_reduce_fusion.1
  16.1 3.4 %fusion.36 = f32[8,256,256]{2,1,0:T(8,128)} fusion(f32[256,8,128]{0,2,1:T(8,128)S(1)} %bitcast.87, bf16[256,1024]{1,0:T(8,128)(2,1)S(1)} %copy-done.7), kind=kOutput, calls=%fused_computation.37 | convolution fusion | flops 806617088 | bytes 3670016 | tf_op jit(solution)/shard_map/thd,shd->hts/dot_general | solution.py:320
  19.6 47.4 %all-gather.6.cloned.1.call-done = bf16[64,128,128]{2,1,0:T(8,128)(2,1)} async-done(((bf16[8,128,128]{2,1,0:T(8,128)(2,1)}), bf16[64,128,128]{2,1,0:T(8,128)(2,1)}) %all-gather.6.cloned.1.call-update) | async-done | bytes 2097168 | tf_op jit(solution)/shard_map/all_gather | solution.py:312
  67.0 2.3 fusion.12
  69.3 1.3 fusion.24
  70.6 1.5 multiply_reduce_fusion
  72.1 0.2 multiply_convert_fusion
  72.3 94.8 %all-gather.4.cloned.1.call-done = bf16[1024,3072]{1,0:T(8,128)(2,1)} async-done(((bf16[1024,384]{1,0:T(8,128)(2,1)}), bf16[1024,3072]{1,0:T(8,128)(2,1)}) %all-gather.4.cloned.1.call-update) | async-done | bytes 6291472 | tf_op jit(solution)/shard_map/all_gather | solution.py:329
  167.1 5.8 %convolution_convert_fusion = bf16[256,3072]{1,0:T(8,128)(2,1)} fusion(bf16[256,1024]{0,1:T(8,128)(2,1)S(1)} %bitcast.88, bf16[1024,3072]{1,0:T(8,128)(2,1)} %all-gather.4.cloned.1.call-done), kind=kOutput, calls=%fused_computation.10 | convolution fusion | flops 1611399168 | bytes 8388608 | tf_op jit(solution)/shard_map/dot_general | solution.py:327
  173.1 0.1 eq.141
  173.4 1.1 reduce-window.20
  174.5 0.2 slice_reduce_fusion
  174.9 0.1 sub.34
  175.2 24.1 %reduce-scatter.2.cloned.1.call-done = bf16[256,768]{1,0:T(8,128)(2,1)} async-done(((bf16[256,3072]{1,0:T(8,128)(2,1)}), bf16[256,768]{1,0:T(8,128)(2,1)}) %reduce-scatter.2.cloned.1.call-update) | async-done | bytes 393232 | tf_op jit(solution)/shard_map/reduce_scatter | solution.py:333
  199.3 1.2 multiply_reduce_fusion.1
  200.5 5.9 %psum.7 = f32[256]{0:T(256)S(1)} all-reduce(f32[256]{0:T(256)S(1)} %multiply_reduce_fusion.1), channel_id=1, replica_groups=mesh['ctx'=8,'head'=4] {'head'}, use_global_device_ids=true, to_apply=%region_12.13 | all-reduce | flops 256 | bytes 2048 | tf_op jit(solution)/shard_map/psum | solution.py:337
  206.5 2.7 convolution_convert_fusion.1
  209.2 40.3 %dispatch.1 = bf16[8,96,3072]{2,1,0:T(8,128)(2,1)} custom-call(bf16[8,96,768]{2,1,0:T(8,128)(2,1)} %bitcast.90), custom_call_target="tpu_custom_call" | custom-call | tf_op jit(solution)/shard_map/dispatch/pallas_call | solution.py:143
  249.5 11.7 %fusion.4 = f32[768,1280]{1,0:T(8,128)} fusion(bf16[768,3072]{1,0:T(8,128)(2,1)} %bitcast.83, bf16[1,3072,1280]{2,1,0:T(8,128)(2,1)} %param.23), kind=kOutput, calls=%fused_computation.4 | convolution fusion | flops 6039797760 | bytes 16515072 | tf_op jit(solution)/shard_map/dot_general | solution.py:362
  261.3 22.0 %fusion.6 = bf16[768,3072]{1,0:T(8,128)(2,1)} fusion(bf16[1,1280,3072]{2,1,0:T(8,128)(2,1)} %param.25, bf16[768,3072]{1,0:T(8,128)(2,1)} %bitcast.84, bf16[1,3072,1280]{2,1,0:T(8,128)(2,1)} %param.24, f32[768,1280]{1,0:T(8,128)} %fusion.4), kind=kOutput, calls=%fused_computation.6 | convolution fusion | flops 12087853056 | bytes 29097984 | tf_op jit(solution)/shard_map/dot_general | solution.py:365
  283.3 43.6 %giveback.1 = bf16[8,96,768]{2,1,0:T(8,128)(2,1)} custom-call(bf16[8,96,3072]{2,1,0:T(8,128)(2,1)} %bitcast.85), custom_call_target="tpu_custom_call" | custom-call | tf_op jit(solution)/shard_map/giveback/pallas_call | solution.py:258
  327.0 1.8 convolution_multiply_fusion.2
  328.8 2.5 fusion.27
  (43 shorter events, 0.9 us)
Async XLA Ops:
  6.5 7.1 %copy-start = (bf16[256,1024]{1,0:T(8,128)(2,1)S(1)}, bf16[256,1024]{1,0:T(8,128)(2,1)}, u32[]{:S(2)}) copy-start(bf16[256,1024]{1,0:T(8,128)(2,1)} %param.15) | copy-start | bytes 1572868
  6.5 9.6 %copy-start.7 = (bf16[256,1024]{1,0:T(8,128)(2,1)S(1)}, bf16[256,1024]{1,0:T(8,128)(2,1)}, u32[]{:S(2)}) copy-start(bf16[256,1024]{1,0:T(8,128)(2,1)} %param.13) | copy-start | bytes 1572868
  6.5 60.5 %all-gather.6.cloned.1.call-start = ((), (), s32[]{:S(2)}) async-start(), calls=%async_computation.3 | async-start | bytes 2359296 | tf_op jit(solution)/shard_map/all_gather | solution.py:312
  15.0 152.1 %all-gather.4.cloned.1.call-start = ((), (), s32[]{:S(2)}) async-start(), calls=%async_computation.1 | async-start | bytes 7077888 | tf_op jit(solution)/shard_map/all_gather | solution.py:329
  15.8 183.5 %reduce-scatter.2.cloned.1.call-start = ((), (), s32[]{:S(2)}) async-start(), calls=%async_computation.2 | async-start | bytes 1966080 | tf_op jit(solution)/shard_map/reduce_scatter | solution.py:333
  67.0 3.6 %copy-start.1 = (f32[8,256,256]{2,1,0:T(8,128)S(1)}, f32[8,256,256]{2,1,0:T(8,128)}, u32[]{:S(2)}) copy-start(f32[8,256,256]{2,1,0:T(8,128)} %fusion.36) | copy-start | bytes 6291460
  69.3 2.8 copy-start.6
  167.1 5.8 %copy-start.4 = (s32[256,2]{0,1:T(2,128)S(1)}, s32[256,2]{0,1:T(2,128)}, u32[]{:S(2)}) copy-start(s32[256,2]{0,1:T(2,128)} %param.21) | copy-start | bytes 6148
  167.1 8.0 %copy-start.5 = (s32[256,2]{0,1:T(2,128)S(1)}, s32[256,2]{0,1:T(2,128)}, u32[]{:S(2)}) copy-start(s32[256,2]{0,1:T(2,128)} %param.22) | copy-start | bytes 6148
  167.1 32.2 %copy-start.2 = (bf16[256,768]{1,0:T(8,128)(2,1)S(1)}, bf16[256,768]{1,0:T(8,128)(2,1)}, u32[]{:S(2)}) copy-start(bf16[256,768]{1,0:T(8,128)(2,1)} %param.19) | copy-start | bytes 1179652
  167.1 39.4 %copy-start.8 = (f32[768]{0:T(1024)S(1)}, f32[768]{0:T(1024)}, u32[]{:S(2)}) copy-start(f32[768]{0:T(1024)} %param.20) | copy-start | bytes 9220
  283.3 45.4 %copy-start.3 = (bf16[256,768]{1,0:T(8,128)(2,1)S(1)}, bf16[256,768]{1,0:T(8,128)(2,1)}, u32[]{:S(2)}) copy-start(bf16[256,768]{1,0:T(8,128)(2,1)} %reduce-scatter.2.cloned.1.call-done) | copy-start | bytes 1179652
Sparse Core Ops, SparseCore 0:
  15.2 51.7 all-gather.5
  69.1 98.0 all-gather.3
  173.1 26.2 reduce-scatter.1

commit v3 on v2

--- a/solution.py
+++ b/solution.py
@@ -269,6 +269,330 @@
     )(partial_value)
 
 
+def attend_kernel(
+    n,
+    heads,
+    q_ref,
+    k_ref,
+    v_ref,
+    allowed_ref,
+    keep_ref,
+    carry_ref,
+    earlier_ref,
+    gain_ref,
+    w_ref,
+    res_ref,
+    hidden_ref,
+    squares_ref,
+    wall,
+    states,
+    attn,
+    headed,
+    acc,
+    mixed,
+    pair,
+    out_x,
+    in_x,
+    sq_own,
+    sq_all,
+    here,
+    w_s,
+    w_r,
+    s_s,
+    s_r,
+    p_s,
+    p_r,
+    x_s,
+    x_r,
+    q_s,
+    q_r,
+):
+    me, chip, core = seat()
+    chips = heads // 2
+    mine, partner = chip * 2 + core, chip * 2 + 1 - core
+    local, size = states.shape[1], HEAD_DIM
+    half, piece = w_ref.shape[0] // 2, w_ref.shape[0] // 4
+    group = n // heads
+    f32 = jnp.float32
+
+    def seat_at(p):
+        return 2 * p - lax.div(p, n // 2) * (4 * p - 2 * n + 1)
+
+    low = lax.div(me, 2)
+    place = low + lax.rem(me, 2) * (n - lax.div(me + 1, 2) - low)
+    ahead = [seat_at(lax.rem(place + 1, n)), seat_at(lax.rem(place + n - 1, n))]
+
+    def origin(way, distance):
+        step = n - distance if way == 0 else distance
+        return seat_at(lax.rem(place + step, n))
+
+    barrier = pltpu.get_barrier_semaphore()
+
+    def tell(ctx, head):
+        pl.semaphore_signal(barrier, inc=1, device_id=(ctx, head), device_id_type=MESH)
+
+    tell(ahead[0], mine)
+    tell(ahead[1], mine)
+    for j in range(1, heads):
+        tell(me, lax.rem(mine + j, heads))
+    pl.semaphore_wait(barrier, heads + 1)
+
+    def w_rows(way, part):
+        return pl.ds(way * half + part * piece, piece)
+
+    def w_first(way, part):
+        rows = w_rows(way, part)
+        return remote(
+            w_ref.at[rows],
+            wall.at[me, rows],
+            w_s.at[way, part, 0],
+            w_r.at[way, part, 0],
+            ahead[way],
+            mine,
+        )
+
+    def w_step(way, part, held, stage):
+        cell = wall.at[origin(way, held), w_rows(way, part)]
+        return remote(
+            cell, cell, w_s.at[way, part, stage], w_r.at[way, part, stage], ahead[way], mine
+        )
+
+    def s_step(way, held, stage):
+        cell = states.at[origin(way, held), pl.ds(way * (local // 2), local // 2)]
+        return remote(cell, cell, s_s.at[way, stage], s_r.at[way, stage], ahead[way], mine)
+
+    for part in range(2):
+        for way in range(2):
+            w_first(way, part).start()
+    own = pltpu.make_async_copy(w_ref, wall.at[me], here)
+    own.start()
+
+    def columns(h):
+        return pl.ds(pl.multiple_of(h * size, size), size)
+
+    def lifted(ref, h):
+        x = ref[:, columns(h)].astype(f32)
+        return x / (1.0 + jnp.exp(-x))
+
+    @pl.loop(0, local)
+    def _(h):
+        kept = lifted(k_ref, h) * keep_ref[...]
+        state = jnp.dot(
+            kept.T, v_ref[:, columns(h)].astype(f32), precision=highest, preferred_element_type=f32
+        )
+        states[me, h] = state.astype(jnp.bfloat16)
+
+    for way in range(2):
+        s_step(way, 0, 0).start()
+
+    @pl.loop(0, local)
+    def _(h):
+        scores = lax.dot_general(
+            lifted(q_ref, h),
+            lifted(k_ref, h),
+            (((1,), (1,)), ((), ())),
+            precision=highest,
+            preferred_element_type=f32,
+        )
+        attn[:, columns(h)] = jnp.dot(
+            scores * allowed_ref[...],
+            v_ref[:, columns(h)].astype(f32),
+            precision=highest,
+            preferred_element_type=f32,
+        )
+
+    acc[...] = jnp.zeros_like(acc)
+
+    def s_stage(stage):
+        for way in range(2):
+            s_step(way, stage + 1, stage).wait_recv()
+
+            @pl.when(stage < n - 2)
+            def _():
+                s_step(way, stage + 1, stage + 1).start()
+
+    def w_stage(stage):
+        for part in range(2):
+            for way in range(2):
+                w_step(way, part, stage + 1, stage).wait_recv()
+
+                @pl.when(stage < n - 2)
+                def _():
+                    w_step(way, part, stage + 1, stage + 1).start()
+
+    early = (n - 2) // 2
+
+    @pl.loop(0, early)
+    def _(t):
+        s_stage(2 * t)
+        s_stage(2 * t + 1)
+        w_stage(t)
+
+    s_stage(n - 2)
+
+    @pl.loop(0, local)
+    def _(h):
+        def add(j, total):
+            return total + earlier_ref[j] * states[j, h].astype(f32)
+
+        state = lax.fori_loop(0, n, add, jnp.zeros((size, size), f32))
+        outside = jnp.dot(
+            lifted(q_ref, h), state, precision=highest, preferred_element_type=f32
+        )
+        full = attn[:, columns(h)] + outside * carry_ref[...]
+        mean_square = jnp.mean(full * full, axis=1, keepdims=True)
+        scaled = full * lax.rsqrt(mean_square + 1e-06) * gain_ref[:, columns(h)]
+        headed[:, columns(h)] = scaled.astype(jnp.bfloat16)
+
+    def project(way, held):
+        src = origin(way, held)
+        rows = pl.ds(way * half, half)
+        acc[src] += jnp.dot(headed[:, rows], wall[src, rows], preferred_element_type=f32)
+
+    own.wait()
+
+    @pl.loop(0, early + 1)
+    def _(held):
+        project(0, held)
+        project(1, held)
+
+    @pl.loop(early, n - 1)
+    def _(stage):
+        w_stage(stage)
+        project(0, stage + 1)
+        project(1, stage + 1)
+
+    mixed[...] = acc[...].astype(jnp.bfloat16)
+
+    def column(j):
+        return lax.rem(chip + j, chips)
+
+    def blocks(head):
+        return pl.ds(head * group, group)
+
+    def swap(j):
+        return remote(
+            mixed.at[blocks(column(j) * 2 + 1 - core)],
+            pair.at[j],
+            p_s.at[j],
+            p_r.at[j],
+            me,
+            partner,
+        )
+
+    def cross(j):
+        return remote(
+            out_x.at[j], in_x.at[j], x_s.at[j], x_r.at[j], me, column(j) * 2 + core
+        )
+
+    for j in list(range(1, chips)) + [0]:
+        swap(j).start()
+
+    def paired(j):
+        swap(j).wait_recv()
+        return acc[blocks(column(j) * 2 + core)] + pair[j].astype(f32)
+
+    for j in range(1, chips):
+        out_x[j] = paired(j).astype(jnp.bfloat16)
+        cross(j).start()
+    total = paired(0) + res_ref[...].astype(f32)
+    hidden_ref[...] = total
+    for j in range(1, chips):
+        cross(j).wait_recv()
+        hidden_ref[...] += in_x[j].astype(f32)
+    ones = jnp.ones((8, hidden_ref.shape[2]), f32)
+    squares = jnp.zeros((8, hidden_ref.shape[1]), f32)
+    for b in range(group):
+        part = hidden_ref[b]
+        squares = squares + lax.dot_general(
+            ones,
+            part * part,
+            (((1,), (1,)), ((), ())),
+            precision=highest,
+            preferred_element_type=f32,
+        )
+    sq_own[...] = squares
+
+    def share(j, to, slot):
+        return remote(sq_own, sq_all.at[slot], q_s.at[j], q_r.at[j], me, to)
+
+    for j in range(1, heads):
+        share(j, lax.rem(mine + j, heads), j).start()
+    for j in range(1, heads):
+        share(j, mine, j).wait_recv()
+        squares = squares + sq_all[j]
+    squares_ref[...] = squares
+
+    for j in range(1, heads):
+        share(j, mine, j).wait_send()
+    for j in range(chips):
+        swap(j).wait_send()
+    for j in range(1, chips):
+        cross(j).wait_send()
+
+    for part in range(2):
+        for way in range(2):
+            w_first(way, part).wait_send()
+
+    @pl.loop(0, n - 1)
+    def _(stage):
+        for way in range(2):
+            s_step(way, stage, stage).wait_send()
+
+    @pl.loop(1, n - 1)
+    def _(stage):
+        for part in range(2):
+            for way in range(2):
+                w_step(way, part, stage, stage).wait_send()
+
+
+def attend(query, key, value, allowed, keep, carry, earlier, gain, weight, residual, n, heads):
+    rows, feats = query.shape
+    width, group = weight.shape[1], n // heads
+    local, chips = feats // HEAD_DIM, heads // 2
+    dma = pltpu.SemaphoreType.DMA
+    bf16, f32 = jnp.bfloat16, jnp.float32
+    vmem = pl.BlockSpec(memory_space=pltpu.VMEM)
+    piece = pltpu.VMEM((chips, group, rows, width), bf16)
+    return pl.pallas_call(
+        functools.partial(attend_kernel, n, heads),
+        out_shape=(
+            jax.ShapeDtypeStruct((group, rows, width), f32),
+            jax.ShapeDtypeStruct((8, rows), f32),
+        ),
+        in_specs=[vmem] * 8 + [pl.BlockSpec(memory_space=pl.ANY), vmem],
+        out_specs=(vmem, vmem),
+        scratch_shapes=[
+            pltpu.VMEM((n,) + weight.shape, bf16),
+            pltpu.VMEM((n, local, HEAD_DIM, HEAD_DIM), bf16),
+            pltpu.VMEM((rows, feats), f32),
+            pltpu.VMEM((rows, feats), bf16),
+            pltpu.VMEM((n, rows, width), f32),
+            pltpu.VMEM((n, rows, width), bf16),
+            piece,
+            piece,
+            piece,
+            pltpu.VMEM((8, rows), f32),
+            pltpu.VMEM((heads, 8, rows), f32),
+            dma,
+            dma((2, 2, n)),
+            dma((2, 2, n)),
+            dma((2, n)),
+            dma((2, n)),
+            dma((chips,)),
+            dma((chips,)),
+            dma((chips,)),
+            dma((chips,)),
+            dma((heads,)),
+            dma((heads,)),
+        ],
+        compiler_params=pltpu.CompilerParams(
+            collective_id=2, has_side_effects=True, vmem_limit_bytes=60 * 1024 * 1024
+        ),
+        name="attend",
+    )(query, key, value, allowed, keep, carry, earlier, gain, weight, residual)
+
+
 def episode_of(positions, lengths):
     starts = jnp.cumsum(lengths) - lengths
     return jnp.sum((starts[None, :] <= positions[:, None]).astype(jnp.int32), axis=1) - 1
@@ -291,53 +615,45 @@
 ):
     tok_rows = query.shape[0]
     head_size = HEAD_DIM
-    heads_local = query.shape[1] // head_size
     own_index = lax.axis_index("ctx")
     ctx_count = lax.axis_size("ctx")
     positions = own_index * tok_rows + jnp.arange(tok_rows, dtype=jnp.int32)
     episode = episode_of(positions, episode_lengths)
     prior = episode_of(positions[:1] - 1, episode_lengths)[0]
     final = episode[-1]
-    lifted_query = jax.nn.silu(query.astype(jnp.float32)).reshape(tok_rows, heads_local, head_size)
-    lifted_key = jax.nn.silu(key.astype(jnp.float32)).reshape(tok_rows, heads_local, head_size)
-    value_rows = value.astype(jnp.float32).reshape(tok_rows, heads_local, head_size)
     keep = (episode == final).astype(jnp.float32)
-    state = jnp.einsum(
-        "shd,she->hde", lifted_key * keep[:, None, None], value_rows, precision=highest
-    )
     finals = episode_of(
         (jnp.arange(ctx_count, dtype=jnp.int32) + 1) * tok_rows - 1, episode_lengths
     )
     earlier = (jnp.arange(ctx_count) < own_index) & (finals == prior)
-    gathered = lax.all_gather(state.astype(jnp.bfloat16), "ctx")
-    carry_state = jnp.sum(
-        jnp.where(earlier[:, None, None, None], gathered.astype(jnp.float32), 0.0), axis=0
+    earlier = jnp.broadcast_to(
+        earlier.astype(jnp.float32)[:, None, None], (ctx_count, 1, head_size)
     )
     order = jnp.arange(tok_rows, dtype=jnp.int32)
     allowed = ((order[:, None] >= order[None, :]) & (episode[:, None] == episode[None, :])).astype(
         jnp.float32
     )
-    scores = jnp.einsum("thd,shd->hts", lifted_query, lifted_key, precision=highest)
-    inside = jnp.einsum("hts,shd->thd", scores * allowed[None], value_rows, precision=highest)
-    outside = jnp.einsum("thd,hde->the", lifted_query, carry_state, precision=highest)
-    attn = inside + outside * (episode == prior).astype(jnp.float32)[:, None, None]
-    mean_square = jnp.mean(attn * attn, axis=2, keepdims=True)
-    scaled = attn * lax.rsqrt(mean_square + 1e-06) * attn_gain.reshape(heads_local, head_size)
-    headed = scaled.reshape(tok_rows, heads_local * head_size).astype(jnp.bfloat16)
-    mixed_part = jnp.dot(
-        headed,
-        lax.all_gather(out_weight, "ctx", axis=1, tiled=True),
-        preferred_element_type=jnp.float32,
-    )
-    width = mixed_part.shape[1]
-    mixed_slice = lax.psum_scatter(
-        mixed_part.astype(jnp.bfloat16), "head", scatter_dimension=1, tiled=True
-    ).astype(jnp.float32)
-    hidden_slice = residual.astype(jnp.float32) + mixed_slice
-    squares = lax.psum(jnp.sum(hidden_slice * hidden_slice, axis=1), "head")
-    normed = (hidden_slice * lax.rsqrt(squares / width + 1e-06)[:, None] * norm_gain).astype(
-        jnp.bfloat16
-    )
+    heads = lax.axis_size("head")
+    col = out_weight.shape[1]
+    width = residual.shape[1] * heads
+    hidden_blocks, squares = attend(
+        query,
+        key,
+        value,
+        allowed,
+        keep[:, None],
+        (episode == prior).astype(jnp.float32)[:, None],
+        earlier,
+        attn_gain[None, :],
+        out_weight,
+        jnp.swapaxes(residual.reshape(tok_rows, -1, col), 0, 1),
+        ctx_count,
+        heads,
+    )
+    hidden_slice = jnp.swapaxes(hidden_blocks, 0, 1).reshape(tok_rows, -1)
+    normed = (
+        hidden_slice * lax.rsqrt(squares[0] / width + 1e-06)[:, None] * norm_gain
+    ).astype(jnp.bfloat16)
     experts_count = gate_weight.shape[0] * ctx_count
     capacity = 3 * tok_rows // experts_count
     flat_ids = expert_ids.reshape(-1)

time: 339 us -> 246 us (0.73)
  waiting for transfers between devices: 167 us -> 0 us
  Pallas kernels: 84 us -> 190 us
  matrix products: 54.2 us -> 39.8 us
  between operations: 14.7 us -> 1.48 us
  blocking collectives: 5.94 us -> 0 us
  local copies, waits for them, and re-layouts: 2.33 us -> 7.98 us
  other arithmetic: 9.59 us -> 5.97 us
    all_gather x2 -> x0, waiting for transfers between devices: 142 us -> none  [the longest x1 94.8 us: on_device(): lax.all_gather(out_weight, 'ctx', axis=1, tiled=True)]
    pallas_call x0 -> x1, Pallas kernels: none -> 106 us  [attend(): pl.pallas_call(functools.partial(attend_kernel, n, heads), out_shape=(jax...]
    reduce_scatter x1 -> x0, waiting for transfers between devices: 24.1 us -> none  [on_device(): lax.psum_scatter(mixed_part.astype(jnp.bfloat16), 'head', scatter_dimensi...]
    dot_general x5 -> x0, matrix products: 13.4 us -> none  [the longest x1 5.81 us: on_device(): jnp.dot(headed, lax.all_gather(out_weight, 'ctx', axis=1, tiled=True), pr...]
    psum x1 -> x0, blocking collectives: 5.94 us -> none  [on_device(): squares = lax.psum(jnp.sum(hidden_slice * hidden_slice, axis=1), 'head')]
    reduce_sum x2 -> x0, other arithmetic: 3.47 us -> none  [the longest x1 2.27 us: on_device(): jnp.sum(jnp.where(earlier[:, None, None, None], gathered.astype(jnp.float...]
  transfers between devices with their start and end apart: 3 -> 0, of which waited for: 3 -> 0; matrix products, arithmetic and copies ran while one was open for 3% -> 0% of each run, Pallas kernels for 0% -> 0%
where the time goes in v3:
time: 246 us; the launch traced here: 245 us
  Pallas kernels  190 us (77%)
  matrix products  39.8 us (16%)
  local copies, waits for them, and re-layouts  7.98 us (3%)
  other arithmetic  5.97 us (2%)
    pallas_call x1, Pallas kernels, attend(): pl.pallas_call(functools.partial(attend_kernel, n, heads), out_shape=(jax...  106 us
    pallas_call x1, Pallas kernels, giveback(): pl.pallas_call(functools.partial(giveback_kernel, n, chips), out_shape=ja...  43.5 us
    pallas_call x1, Pallas kernels, dispatch(): pl.pallas_call(functools.partial(dispatch_kernel, n, chips), out_shape=ja...  39.7 us
    dot_general x1, matrix products, on_device(): jnp.dot(gated, down_weight[0], preferred_element_type=jnp.float32)  22.1 us
    dot_general x1, matrix products, on_device(): gate = jnp.dot(flat, gate_weight[0], preferred_element_type=jnp.float32)  11.7 us

profile of v3, /device:TPU:0, one launch (start us, length us, event | category | flops | bytes accessed | tf_op | source)
XLA Modules:
  0.0 244.8 jit_solution(9235307828150898451)
XLA Ops:
  0.0 0.5 slice.30
  1.2 0.8 reduce-window.19
  2.0 1.4 fusion.32
  3.4 0.1 convert_reduce_fusion
  3.5 0.6 slice.29
  4.8 0.7 compare_convert_fusion
  5.4 0.8 copy.46.keep_ref
  6.2 0.8 copy.47.carry_ref
  7.0 0.2 convert_reduce_fusion.1
  7.2 0.7 broadcast_in_dim.4.earlier_ref
  7.9 0.8 fusion.29.allowed_ref
  8.7 1.2 copy.44
  9.8 0.9 copy.45
  10.8 106.4 %attend.1 = (f32[2,256,384]{2,1,0:T(8,128)}, f32[8,256]{1,0:T(8,128)}) custom-call(bf16[256,1024]{1,0:T(8,128)(2,1)} %q_ref.1, bf16[256,1024]{1,0:T(8,128)(2,1)} %k_ref.1, bf16[256,1024]{1,0:T(8,128)(2,1)} %v_ref.1, f32[256,256]{1,0:T(8,128)} %fusion.29.allowed_ref, f32[256,1]{1,0:T(8,128)} %copy.46.keep_ref, f32[256,1]{1,0:T(8,128)} %copy.47.carry_ref, ...), custom_call_target="tpu_custom_call" | custom-call | tf_op jit(solution)/shard_map/attend/pallas_call | solution.py:557
  117.1 1.4 copy.48
  118.5 0.7 add_rsqrt_fusion
  119.2 0.1 copy.49
  119.4 0.1 eq.145
  119.5 1.1 reduce-window.20
  120.7 0.2 slice_reduce_fusion
  120.9 0.1 eq.141
  121.1 0.1 fusion.30
  121.2 0.1 sub.34
  121.3 0.1 copy.51
  121.4 1.7 convolution_convert_fusion
  123.1 39.7 %dispatch.1 = bf16[8,96,3072]{2,1,0:T(8,128)(2,1)} custom-call(bf16[8,96,768]{2,1,0:T(8,128)(2,1)} %bitcast.56), custom_call_target="tpu_custom_call" | custom-call | tf_op jit(solution)/shard_map/dispatch/pallas_call | solution.py:143
  162.8 11.7 %fusion.4 = f32[768,1280]{1,0:T(8,128)} fusion(bf16[768,3072]{1,0:T(8,128)(2,1)} %bitcast.53, bf16[1,3072,1280]{2,1,0:T(8,128)(2,1)} %param.23), kind=kOutput, calls=%fused_computation.4 | convolution fusion | flops 6039797760 | bytes 16515072 | tf_op jit(solution)/shard_map/dot_general | solution.py:678
  174.6 22.1 %fusion.6 = bf16[768,3072]{1,0:T(8,128)(2,1)} fusion(bf16[1,1280,3072]{2,1,0:T(8,128)(2,1)} %param.25, bf16[768,3072]{1,0:T(8,128)(2,1)} %bitcast.54, bf16[1,3072,1280]{2,1,0:T(8,128)(2,1)} %param.24, f32[768,1280]{1,0:T(8,128)} %fusion.4), kind=kOutput, calls=%fused_computation.6 | convolution fusion | flops 12087853056 | bytes 29097984 | tf_op jit(solution)/shard_map/dot_general | solution.py:681
  196.6 43.5 %giveback.1 = bf16[8,96,768]{2,1,0:T(8,128)(2,1)} custom-call(bf16[8,96,3072]{2,1,0:T(8,128)(2,1)} %bitcast.55), custom_call_target="tpu_custom_call" | custom-call | tf_op jit(solution)/shard_map/giveback/pallas_call | solution.py:258
  240.2 1.8 convolution_multiply_fusion.1
  242.0 0.3 copy.52
  242.2 2.5 %fusion.17 = bf16[256,768]{1,0:T(8,128)(2,1)} fusion(f32[256,768]{1,0:T(8,128)S(1)} %copy.52, f32[256,768]{1,0:T(8,128)S(1)} %convolution_multiply_fusion.1, bf16[768,768]{1,0:T(8,128)(2,1)} %bitcast.50, s32[256]{0:T(256)S(1)} %bitcast.61, f32[256]{0:T(256)S(1)} %bitcast.66), kind=kOutput, calls=%fused_computation.14 | convolution fusion | flops 302972928 | bytes 3147776 | tf_op jit(solution)/shard_map/dot_general | solution.py:691
  (18 shorter events, 0.1 us)
Async XLA Ops:
  0.0 119.2 %copy-start = (s32[256,2]{0,1:T(2,128)S(1)}, s32[256,2]{0,1:T(2,128)}, u32[]{:S(2)}) copy-start(s32[256,2]{0,1:T(2,128)} %param.21) | copy-start | bytes 6148
  0.0 121.4 %copy-start.2 = (f32[768]{0:T(1024)S(1)}, f32[768]{0:T(1024)}, u32[]{:S(2)}) copy-start(f32[768]{0:T(1024)} %param.20) | copy-start | bytes 9220
  196.6 43.5 %copy-start.1 = (s32[256,2]{0,1:T(2,128)S(1)}, s32[256,2]{0,1:T(2,128)}, u32[]{:S(2)}) copy-start(s32[256,2]{0,1:T(2,128)} %param.22) | copy-start | bytes 6148

commit v4 on v3

--- a/solution.py
+++ b/solution.py
@@ -54,7 +54,26 @@
 
 
 def dispatch_kernel(
-    n, chips, out_ref, full_ref, here, a_s, a_r, p_s, p_r, x_s, x_r, f_s, f_r
+    n,
+    chips,
+    pair,
+    out_ref,
+    gate_ref,
+    up_ref,
+    gated_ref,
+    full_ref,
+    gate_w,
+    up_w,
+    here,
+    w_s,
+    a_s,
+    a_r,
+    p_s,
+    p_r,
+    x_s,
+    x_r,
+    f_s,
+    f_r,
 ):
     me, chip, core = seat()
     width = out_ref.shape[2]
@@ -64,37 +83,41 @@
         return full_ref.at[block, :, pl.ds(pl.multiple_of(head * width, 128), width)]
 
     greet(n, chips, True)
-    own = pltpu.make_async_copy(out_ref.at[me], cell(me, mine), here)
+    own = pltpu.make_async_copy(out_ref.at[me], cell(0, mine), here)
     own.start()
+    weights = [
+        pltpu.make_async_copy(gate_ref, gate_w, w_s.at[0]),
+        pltpu.make_async_copy(up_ref, up_w, w_s.at[1]),
+    ]
 
     def sent(i):
         to = lax.rem(me + i, n)
-        return remote(out_ref.at[to], cell(me, mine), a_s.at[i], a_r.at[i], to, mine)
+        return remote(out_ref.at[to], cell(i, mine), a_s.at[i], a_r.at[i], to, mine)
 
     @pl.loop(1, n)
     def _(i):
         sent(i).start()
 
-    def block_of(i):
-        return lax.rem(me - i + n, n)
+    for copy in weights:
+        copy.start()
 
     def arrived(i):
-        return remote(out_ref.at[me], cell(block_of(i), mine), a_s.at[i], a_r.at[i], me, mine)
+        return remote(out_ref.at[me], cell(i, mine), a_s.at[i], a_r.at[i], me, mine)
 
     def to_partner(i, head):
-        b = cell(block_of(i), head)
+        b = cell(i, head)
         return remote(b, b, p_s.at[i], p_r.at[i], me, partner)
 
     def to_chip(i, j):
-        b = cell(block_of(i), mine)
+        b = cell(i, mine)
         return remote(b, b, x_s.at[j, i], x_r.at[j, i], me, lax.rem(chip + j, chips) * 2 + core)
 
     def from_chip(i, j):
-        b = cell(block_of(i), lax.rem(chip - j + chips, chips) * 2 + core)
+        b = cell(i, lax.rem(chip - j + chips, chips) * 2 + core)
         return remote(b, b, x_s.at[j, i], x_r.at[j, i], me, mine)
 
     def forward(i, j, which):
-        b = cell(block_of(i), lax.rem(chip - j + chips, chips) * 2 + which)
+        b = cell(i, lax.rem(chip - j + chips, chips) * 2 + which)
         return remote(b, b, f_s.at[j, i], f_r.at[j, i], me, partner)
 
     def spread(i):
@@ -107,6 +130,24 @@
             from_chip(i, j).wait_recv()
             forward(i, j, core).start()
 
+    def multiply(slot):
+        rows = full_ref[pl.ds(slot, pair)]
+        rows = rows.reshape(pair * rows.shape[1], rows.shape[2])
+        columns = gate_w.shape[1]
+        tile = 640 if columns % 640 == 0 else columns
+        for start in range(0, columns, tile):
+            part = slice(start, start + tile)
+            gate = jnp.dot(rows, gate_w[:, part], preferred_element_type=jnp.float32)
+            up = jnp.dot(rows, up_w[:, part], preferred_element_type=jnp.float32)
+            gated = (gate / (1.0 + jnp.exp(-gate)) * up).astype(jnp.bfloat16)
+            gated_ref[pl.ds(slot, pair), :, part] = gated.reshape(pair, -1, tile)
+
+    def complete(slot):
+        for e in range(pair):
+            to_partner(slot + e, partner).wait_recv()
+            for j in range(1, chips):
+                forward(slot + e, j, 1 - core).wait_recv()
+
     own.wait()
     spread(0)
 
@@ -119,15 +160,28 @@
         def _():
             relay(i - 2)
 
+        @pl.when(i == 4)
+        def _():
+            for copy in weights:
+                copy.wait()
+
+        @pl.when((i >= 3 + pair) & (lax.rem(i, pair) == pair - 1))
+        def _():
+            complete(i - 3 - pair)
+            multiply(i - 3 - pair)
+
     relay(n - 2)
     relay(n - 1)
 
+    @pl.loop(0, 4 // pair)
+    def _(t):
+        complete(n - 4 + t * pair)
+        multiply(n - 4 + t * pair)
+
     @pl.loop(0, n)
     def _(i):
-        to_partner(i, partner).wait_recv()
         to_partner(i, mine).wait_send()
         for j in range(1, chips):
-            forward(i, j, 1 - core).wait_recv()
             forward(i, j, core).wait_send()
             to_chip(i, j).wait_send()
 
@@ -136,24 +190,31 @@
         sent(i).wait_send()
 
 
-def dispatch(outgoing, n, heads):
+def dispatch(outgoing, gate, up, n, heads):
     chips = heads // 2
     rows, width = outgoing.shape[1:]
     dma = pltpu.SemaphoreType.DMA
     return pl.pallas_call(
-        functools.partial(dispatch_kernel, n, chips),
-        out_shape=jax.ShapeDtypeStruct((n, rows, width * heads), outgoing.dtype),
-        in_specs=[pl.BlockSpec(memory_space=pl.ANY)],
-        out_specs=pl.BlockSpec(memory_space=pl.ANY),
-        scratch_shapes=[dma, dma((n,)), dma((n,)), dma((n,)), dma((n,))]
+        functools.partial(dispatch_kernel, n, chips, 2 if rows % 16 == 0 else 1),
+        out_shape=jax.ShapeDtypeStruct((n, rows, gate.shape[1]), outgoing.dtype),
+        in_specs=[pl.BlockSpec(memory_space=pl.ANY)] * 3,
+        out_specs=pl.BlockSpec(memory_space=pltpu.VMEM),
+        scratch_shapes=[
+            pltpu.VMEM((n, rows, width * heads), outgoing.dtype),
+            pltpu.VMEM(gate.shape, gate.dtype),
+            pltpu.VMEM(up.shape, up.dtype),
+        ]
+        + [dma, dma((2,)), dma((n,)), dma((n,)), dma((n,)), dma((n,))]
         + [dma((chips, n))] * 4,
-        compiler_params=pltpu.CompilerParams(collective_id=0, has_side_effects=True),
+        compiler_params=pltpu.CompilerParams(
+            collective_id=0, has_side_effects=True, vmem_limit_bytes=60 * 1024 * 1024
+        ),
         name="dispatch",
-    )(outgoing)
+    )(outgoing, gate, up)
 
 
 def giveback_kernel(
-    n, chips, part_ref, ret_ref, own, pair, out_x, in_x, total, here, l_s, p_s, p_r, x_s, x_r, a_s, a_r
+    n, chips, batch, gated_ref, down_ref, ret_ref, part_ref, pair, out_x, in_x, total, here, p_s, p_r, x_s, x_r, a_s, a_r
 ):
     me, chip, core = seat()
     rows, width = ret_ref.shape[1:]
@@ -168,14 +229,9 @@
     def column(j):
         return lax.rem(chip + j, chips)
 
-    def load(i, j):
-        return pltpu.make_async_copy(
-            cell(block_of(i), column(j) * 2 + core), own.at[i, j], l_s.at[j, i]
-        )
-
     def swap(i, j):
         return remote(
-            cell(block_of(i), column(j) * 2 + 1 - core),
+            cell(n - 1 - i, column(j) * 2 + 1 - core),
             pair.at[i, j],
             p_s.at[j, i],
             p_r.at[j, i],
@@ -195,16 +251,23 @@
 
     greet(n, chips, True)
 
-    @pl.loop(0, n)
-    def _(i):
-        for j in list(range(1, chips)) + [0]:
-            swap(i, j).start()
-            load(i, j).start()
+    def produce(t):
+        slots = pl.ds(n - (t + 1) * batch, batch)
+        rows_in = gated_ref[slots].reshape(batch * rows, gated_ref.shape[2])
+        tile = 768
+        for start in range(0, part_ref.shape[2], tile):
+            part = slice(start, start + tile)
+            value = jnp.dot(rows_in, down_ref[:, part], preferred_element_type=jnp.float32)
+            part_ref[slots, :, part] = value.astype(jnp.bfloat16).reshape(batch, rows, tile)
+        for e in range(batch):
+            for j in list(range(1, chips)) + [0]:
+                swap(t * batch + e, j).start()
 
     def paired(i, j):
-        load(i, j).wait()
         swap(i, j).wait_recv()
-        return own[i, j].astype(jnp.float32) + pair[i, j].astype(jnp.float32)
+        head = pl.multiple_of((column(j) * 2 + core) * width, 128)
+        own = part_ref[n - 1 - i, :, pl.ds(head, width)]
+        return own.astype(jnp.float32) + pair[i, j].astype(jnp.float32)
 
     def first(i):
         for j in range(1, chips):
@@ -218,19 +281,28 @@
             acc = acc + in_x[i, j].astype(jnp.float32)
         total[i] = acc.astype(jnp.bfloat16)
 
-    first(0)
-    first(1)
-
-    @pl.loop(0, n - 1)
-    def _(i):
-        @pl.when(i + 2 < n)
+    groups = n // batch
+    produce(0)
+
+    @pl.loop(0, groups)
+    def _(t):
+        @pl.when(t + 1 < groups)
         def _():
-            first(i + 2)
-
+            produce(t + 1)
+
+        for e in range(batch):
+            first(t * batch + e)
+
+        @pl.when(t >= 1)
+        def _():
+            for e in range(batch):
+                second((t - 1) * batch + e)
+                home((t - 1) * batch + e).start()
+
+    for i in range(n - batch, n):
         second(i)
-        home(i).start()
-
-    second(n - 1)
+        if i < n - 1:
+            home(i).start()
     keep = pltpu.make_async_copy(total.at[n - 1], ret_ref.at[me], here)
     keep.start()
 
@@ -250,23 +322,31 @@
     keep.wait()
 
 
-def giveback(partial_value, n, heads):
+def giveback(gated, down, n, heads):
     chips = heads // 2
-    rows, width = partial_value.shape[1], partial_value.shape[2] // heads
+    rows, width = gated.shape[1], down.shape[1] // heads
     dma = pltpu.SemaphoreType.DMA
     piece = pltpu.VMEM((n, chips, rows, width), jnp.bfloat16)
     return pl.pallas_call(
-        functools.partial(giveback_kernel, n, chips),
+        functools.partial(giveback_kernel, n, chips, 2 if rows % 16 == 0 else 1),
         out_shape=jax.ShapeDtypeStruct((n, rows, width), jnp.bfloat16),
-        in_specs=[pl.BlockSpec(memory_space=pl.ANY)],
+        in_specs=[pl.BlockSpec(memory_space=pltpu.VMEM)] * 2,
         out_specs=pl.BlockSpec(memory_space=pl.ANY),
-        scratch_shapes=[piece, piece, piece, piece, pltpu.VMEM((n, rows, width), jnp.bfloat16)]
+        scratch_shapes=[
+            pltpu.VMEM((n, rows, width * heads), jnp.bfloat16),
+            piece,
+            piece,
+            piece,
+            pltpu.VMEM((n, rows, width), jnp.bfloat16),
+        ]
         + [dma]
-        + [dma((chips, n))] * 5
+        + [dma((chips, n))] * 4
         + [dma((n,))] * 2,
-        compiler_params=pltpu.CompilerParams(collective_id=1, has_side_effects=True),
+        compiler_params=pltpu.CompilerParams(
+            collective_id=1, has_side_effects=True, vmem_limit_bytes=60 * 1024 * 1024
+        ),
         name="giveback",
-    )(partial_value)
+    )(gated, down)
 
 
 def attend_kernel(
@@ -673,17 +753,8 @@
     )
     raw_weights = route_weights.astype(jnp.float32)
     share = raw_weights / jnp.sum(raw_weights, axis=1, keepdims=True)
-    full_rows = dispatch(outgoing, ctx_count, lax.axis_size("head"))
-    flat = full_rows.reshape(-1, full_rows.shape[2])
-    gate = jnp.dot(flat, gate_weight[0], preferred_element_type=jnp.float32)
-    up = jnp.dot(flat, up_weight[0], preferred_element_type=jnp.float32)
-    gated = (jax.nn.silu(gate) * up).astype(jnp.bfloat16)
-    partial_value = jnp.dot(gated, down_weight[0], preferred_element_type=jnp.float32).astype(
-        jnp.bfloat16
-    )
-    returned = giveback(
-        partial_value.reshape(full_rows.shape), ctx_count, lax.axis_size("head")
-    )
+    gated = dispatch(outgoing, gate_weight[0], up_weight[0], ctx_count, heads)
+    returned = giveback(gated, down_weight[0], ctx_count, heads)
     returned = returned.reshape(-1, returned.shape[2])
     moe = 0.0
     for k in range(2):

time: 246 us -> 224 us (0.911)
  matrix products: 39.8 us -> 4.7 us
  Pallas kernels: 190 us -> 202 us
    dot_general x2 -> x0, matrix products: 33.8 us -> none  [the longest x1 22.1 us: on_device(): jnp.dot(gated, down_weight[0], preferred_element_type=jnp.float32)]
    pallas_call x2, Pallas kernels: 83.2 us -> 95.5 us  [the longest x1 48.3 us: giveback(): pl.pallas_call(functools.partial(giveback_kernel, n, chips, 2 if rows % 1...]
where the time goes in v4:
time: 224 us; the launch traced here: 223 us
  Pallas kernels  202 us (90%)
  local copies, waits for them, and re-layouts  8.99 us (4%)
  other arithmetic  5.97 us (3%)
  matrix products  4.7 us (2%)
    pallas_call x1, Pallas kernels, attend(): pl.pallas_call(functools.partial(attend_kernel, n, heads), out_shape=(jax...  106 us
    pallas_call x1, Pallas kernels, giveback(): pl.pallas_call(functools.partial(giveback_kernel, n, chips, 2 if rows % 1...  48.3 us
    pallas_call x1, Pallas kernels, dispatch(): pl.pallas_call(functools.partial(dispatch_kernel, n, chips, 2 if rows % 1...  47.2 us

profile of v4, /device:TPU:0, one launch (start us, length us, event | category | flops | bytes accessed | tf_op | source)
XLA Modules:
  0.0 223.0 jit_solution(8314968302821144895)
XLA Ops:
  0.0 0.5 slice.30
  1.2 0.8 reduce-window.19
  2.0 1.4 fusion.15
  3.4 0.1 convert_reduce_fusion
  3.5 0.6 slice.29
  4.7 0.7 compare_convert_fusion
  5.4 0.8 copy.46.keep_ref
  6.2 0.8 copy.47.carry_ref
  7.0 0.2 convert_reduce_fusion.1
  7.2 0.7 broadcast_in_dim.4.earlier_ref
  7.9 0.8 fusion.12.allowed_ref
  8.7 1.2 copy.44
  9.8 0.9 copy.45
  10.8 106.3 %attend.1 = (f32[2,256,384]{2,1,0:T(8,128)}, f32[8,256]{1,0:T(8,128)}) custom-call(bf16[256,1024]{1,0:T(8,128)(2,1)} %q_ref.1, bf16[256,1024]{1,0:T(8,128)(2,1)} %k_ref.1, bf16[256,1024]{1,0:T(8,128)(2,1)} %v_ref.1, f32[256,256]{1,0:T(8,128)} %fusion.12.allowed_ref, f32[256,1]{1,0:T(8,128)} %copy.46.keep_ref, f32[256,1]{1,0:T(8,128)} %copy.47.carry_ref, ...), custom_call_target="tpu_custom_call" | custom-call | tf_op jit(solution)/shard_map/attend/pallas_call | solution.py:637
  117.1 0.0 copy-start.1
  117.1 1.4 copy.48
  118.5 0.7 add_rsqrt_fusion
  119.2 0.1 copy.49
  119.4 0.1 eq.145
  119.5 1.1 reduce-window.20
  120.7 0.2 slice_reduce_fusion
  120.9 0.1 eq.141
  121.1 0.1 fusion.13
  121.2 0.1 sub.34
  121.3 0.1 copy.51
  121.4 1.6 convolution_convert_fusion
  123.1 47.2 %dispatch.1.gated_ref = bf16[8,96,1280]{2,1,0:T(8,128)(2,1)} custom-call(bf16[8,96,768]{2,1,0:T(8,128)(2,1)} %bitcast.38, bf16[3072,1280]{1,0:T(8,128)(2,1)} %bitcast.33, bf16[3072,1280]{1,0:T(8,128)(2,1)} %bitcast.34), custom_call_target="tpu_custom_call" | custom-call | tf_op jit(solution)/shard_map/dispatch/pallas_call | solution.py:197
  170.3 48.3 %giveback.1 = bf16[8,96,768]{2,1,0:T(8,128)(2,1)} custom-call(bf16[8,96,1280]{2,1,0:T(8,128)(2,1)} %dispatch.1.gated_ref, bf16[1280,3072]{1,0:T(8,128)(2,1)} %bitcast.35), custom_call_target="tpu_custom_call" | custom-call | tf_op jit(solution)/shard_map/giveback/pallas_call | solution.py:330
  218.6 1.8 convolution_multiply_fusion.1
  220.4 0.3 copy.52
  220.7 1.0 copy-done
  221.7 1.3 fusion.2
  (18 shorter events, 0.1 us)
Async XLA Ops:
  117.1 2.1 copy-start.1
  117.1 4.3 %copy-start.3 = (f32[768]{0:T(1024)S(1)}, f32[768]{0:T(1024)}, u32[]{:S(2)}) copy-start(f32[768]{0:T(1024)} %param.20) | copy-start | bytes 9220
  170.3 48.3 %copy-start.2 = (s32[256,2]{0,1:T(2,128)S(1)}, s32[256,2]{0,1:T(2,128)}, u32[]{:S(2)}) copy-start(s32[256,2]{0,1:T(2,128)} %param.22) | copy-start | bytes 6148
  220.4 1.3 copy-start
